TPU v7x, 256 devices: a whole 4x4x8 slice. The times are simulated.
256 devices in a mesh: dp: 16 (over x, y), tensor: 16 (over z, core).
Axes of the slice: x: 4, y: 4, z: 8, core: 2. Of those that a mesh axis runs over, the one named last changes fastest.
Arguments:
- tokens: bfloat16 [4096, 2048], P(('dp', 'tensor')), may hold values from -6 to 6
- attn_gain: bfloat16 [2048], replicated, may hold values from 0.099609375 to 1.8984375
- mlp_gain: bfloat16 [2048], replicated, may hold values from 0.099609375 to 1.8984375
- project_in: bfloat16 [3, 2048, 2048], P(None, None, 'tensor'), may hold values from -6 to 6
- project_out: bfloat16 [2048, 2048], P('tensor'), may hold values from -0.125 to 0.125
- gate_up: bfloat16 [2, 2048, 8192], P(None, None, 'tensor'), may hold values from -0.125 to 0.125
- project_down: bfloat16 [8192, 2048], P('tensor'), may hold values from -0.0625 to 0.0625
- kv_cache: bfloat16 [2, 65536, 2048], P(None, 'dp', 'tensor'), may hold values from -10 to 10
- lengths: int32 [4096], replicated, may hold values from 1 to 1024, as said below
- owners: int32 [4096], replicated, may hold values from 0 to 15, as said below
- cache_start: int32 [4096], replicated, may hold values from 0 to 4094, as said below
Outputs:
- hidden_states: bfloat16 [4096, 2048], P(('dp', 'tensor'))
- log_sum_exp: float32 [4096, 32], P('dp', 'tensor')
- kv_updated: bfloat16 [2, 65536, 2048], P(None, 'dp', 'tensor')
Inputs may be any that keep to these rules, and one draw needn't show every extreme that they name: `lengths`: the largest length is exactly 1024 in every draw. `owners`: in each aligned block of 256 requests (those of one dp index) exactly 128 requests name another owner than the block's index and the rest name the block's index; no other owner is named by more than 9 requests of one block, and in every block one owner is named by exactly 9. The requests of one owner occupy disjoint ranges of positions from cache_start to cache_start + length, the last of these (the position for the new token) included, all within that owner's 4096 positions.
All inputs are finite; a program needn't handle non-finite values.
Results may differ from a plain program's by a relative error of at most 0.008.
Values may be sent and summed in bfloat16 or wider, within the bound.
A program may use at most 64 MiB of HBM per device.

v0:
```python
import math

import jax
import jax.numpy as jnp
from jax import lax
from jax.sharding import PartitionSpec as P

MOST = 4
HD = 64


NORM_EPS = 1e-05
ROPE_BASE = 130000.0
MASK_LOW = -1e30


def scaled_norm(values, scales):
    wide = values.astype(jnp.float32)
    factor = lax.rsqrt(jnp.mean(wide * wide, axis=-1, keepdims=True) + NORM_EPS)
    return (wide * factor * scales.astype(jnp.float32)).astype(jnp.bfloat16)


def rotate(values, positions, head_size):
    half_size = head_size // 2
    freqs = ROPE_BASE ** (-(jnp.arange(half_size, dtype=jnp.float32) * 2.0 / head_size))
    angles = positions.astype(jnp.float32)[:, None] * freqs[None, :]
    cosine = jnp.cos(angles)[:, None, :]
    sine = jnp.sin(angles)[:, None, :]
    first = values[..., :half_size]
    second = values[..., half_size:]
    return jnp.concatenate(
        [first * cosine - second * sine, second * cosine + first * sine], axis=-1
    )


def expand_hidden(normed_rows, gate_up):
    both = jnp.einsum("rd,cdf->rcf", normed_rows, gate_up, preferred_element_type=jnp.float32)
    return (jax.nn.silu(both[:, 0]) * both[:, 1]).astype(jnp.bfloat16)


def partials(kv_cache, queries, starts, seg_spans, head_size):
    query_count = queries.shape[0]
    feat_width = queries.shape[1]
    heads_local = feat_width // head_size
    cache_rows = kv_cache.shape[1]
    block_rows = min(512, cache_rows)
    ends = jnp.where(seg_spans > 0, starts + seg_spans, 0)
    block_count = (jnp.max(ends) + block_rows - 1) // block_rows
    query_heads = queries.reshape(query_count, heads_local, head_size)
    scale = 1.0 / math.sqrt(head_size)
    finish = starts + seg_spans

    def advance(step_index, carry):
        running_top, running_sum, running_out = carry
        first_row = step_index * block_rows
        window = lax.dynamic_slice_in_dim(kv_cache, first_row, block_rows, 1)
        key_block = window[0].reshape(block_rows, heads_local, head_size)
        value_block = window[1].reshape(block_rows, heads_local, head_size).astype(jnp.float32)
        scores = (
            jnp.einsum("qhe,phe->qhp", query_heads, key_block, preferred_element_type=jnp.float32)
            * scale
        )
        position = first_row + jnp.arange(block_rows)
        live = (position[None, :] >= starts[:, None]) & (position[None, :] < finish[:, None])
        live = live[:, None, :]
        masked = jnp.where(live, scores, MASK_LOW)
        new_top = jnp.maximum(running_top, jnp.max(masked, axis=-1))
        weights = jnp.where(live, jnp.exp(masked - new_top[..., None]), 0.0)
        factor = jnp.exp(running_top - new_top)
        running_sum = running_sum * factor + jnp.sum(weights, axis=-1)
        running_out = running_out * factor[..., None] + jnp.einsum(
            "qhp,phe->qhe", weights, value_block, precision=lax.Precision.HIGHEST
        )
        return (new_top, running_sum, running_out)

    initial = (
        jnp.full((query_count, heads_local), MASK_LOW, jnp.float32),
        jnp.zeros((query_count, heads_local), jnp.float32),
        jnp.zeros((query_count, heads_local, head_size), jnp.float32),
    )
    final_top, final_sum, final_out = lax.fori_loop(0, block_count, advance, initial)
    return (final_out.reshape(query_count, feat_width), final_top, final_sum)


def on_device(
    tokens,
    attn_gain,
    mlp_gain,
    project_in,
    project_out,
    gate_up,
    project_down,
    kv_cache,
    lengths,
    owners,
    cache_start,
):
    groups = lax.axis_size("dp")
    my_index = lax.axis_index("dp")
    tok_rows = tokens.shape[0]
    request_count = tok_rows * lax.axis_size("tensor")
    feat_width = project_in.shape[2]
    head_size = HD
    heads_local = feat_width // head_size
    cache_rows = kv_cache.shape[1]
    capacity = max(MOST, (request_count // 2 + groups - 2) // (groups - 1))
    slot_count = groups * capacity
    gathered = lax.all_gather(tokens, "tensor", axis=0, tiled=True)
    normed = scaled_norm(gathered, attn_gain)
    projected = jnp.einsum("rd,cde->rce", normed, project_in, preferred_element_type=jnp.float32)
    my_length = lax.dynamic_slice_in_dim(lengths, my_index * request_count, request_count)
    my_owner = lax.dynamic_slice_in_dim(owners, my_index * request_count, request_count)
    my_start = lax.dynamic_slice_in_dim(cache_start, my_index * request_count, request_count)
    queries = (
        rotate(projected[:, 0].reshape(request_count, heads_local, head_size), my_length, head_size)
        .astype(jnp.bfloat16)
        .reshape(request_count, feat_width)
    )
    keys_new = (
        rotate(projected[:, 1].reshape(request_count, heads_local, head_size), my_length, head_size)
        .astype(jnp.bfloat16)
        .reshape(request_count, feat_width)
    )
    values_new = projected[:, 2].astype(jnp.bfloat16)
    packed = jnp.concatenate([queries, keys_new, values_new], axis=1)
    remote = my_owner != my_index
    target = (my_owner[:, None] == jnp.arange(groups)[None, :]) & remote[:, None]
    target_int = target.astype(jnp.int32)
    send_rank = jnp.sum((jnp.cumsum(target_int, axis=0) - target_int) * target_int, axis=1)
    send_place = jnp.where(remote, my_owner * capacity + send_rank, -1)
    selector = (jnp.arange(slot_count)[:, None] == send_place[None, :]).astype(jnp.bfloat16)
    outgoing = jnp.dot(selector, packed, preferred_element_type=jnp.float32).astype(jnp.bfloat16)
    outgoing = outgoing.reshape(groups, capacity, 3 * feat_width)
    arrived = lax.all_to_all(outgoing, "dp", split_axis=0, concat_axis=0, tiled=True).reshape(
        slot_count, 3 * feat_width
    )
    owner_blocks = owners.reshape(groups, request_count)
    bound_here = (owner_blocks == my_index) & (jnp.arange(groups)[:, None] != my_index)
    here_int = bound_here.astype(jnp.int32)
    in_rank = jnp.cumsum(here_int, axis=1) - here_int
    matched = bound_here[:, None, :] & (in_rank[:, None, :] == jnp.arange(capacity)[None, :, None])
    in_length = jnp.sum(
        jnp.where(matched, lengths.reshape(groups, request_count)[:, None, :], 0), axis=-1
    ).reshape(slot_count)
    in_start = jnp.sum(
        jnp.where(matched, cache_start.reshape(groups, request_count)[:, None, :], 0), axis=-1
    ).reshape(slot_count)
    in_live = jnp.any(matched, axis=-1).reshape(slot_count)
    in_span = jnp.where(in_live, in_length, 0)
    home_span = jnp.where(remote, 0, my_length)
    arrived_queries = arrived[:, :feat_width]
    joint_out, joint_top, joint_sum = partials(
        kv_cache,
        jnp.concatenate([queries, arrived_queries], axis=0),
        jnp.concatenate([my_start, in_start]),
        jnp.concatenate([home_span, in_span]),
        head_size,
    )
    home_out, far_out = (joint_out[:request_count], joint_out[request_count:])
    home_top, far_top = (joint_top[:request_count], joint_top[request_count:])
    home_sum, far_sum = (joint_sum[:request_count], joint_sum[request_count:])
    back_out, back_top, back_sum = (
        lax.all_to_all(
            far_out.reshape(groups, capacity, feat_width),
            "dp",
            split_axis=0,
            concat_axis=0,
            tiled=True,
        ),
        lax.all_to_all(
            far_top.reshape(groups, capacity, heads_local),
            "dp",
            split_axis=0,
            concat_axis=0,
            tiled=True,
        ),
        lax.all_to_all(
            far_sum.reshape(groups, capacity, heads_local),
            "dp",
            split_axis=0,
            concat_axis=0,
            tiled=True,
        ),
    )
    fetch_index = jnp.clip(send_place, 0, slot_count - 1)
    part_out = jnp.where(
        remote[:, None],
        jnp.take(back_out.reshape(slot_count, feat_width), fetch_index, axis=0),
        home_out,
    )
    part_top = jnp.where(
        remote[:, None],
        jnp.take(back_top.reshape(slot_count, heads_local), fetch_index, axis=0),
        home_top,
    )
    part_sum = jnp.where(
        remote[:, None],
        jnp.take(back_sum.reshape(slot_count, heads_local), fetch_index, axis=0),
        home_sum,
    )
    query_heads = queries.reshape(request_count, heads_local, head_size).astype(jnp.float32)
    key_heads = keys_new.reshape(request_count, heads_local, head_size).astype(jnp.float32)
    value_heads = values_new.reshape(request_count, heads_local, head_size).astype(jnp.float32)
    own_score = jnp.sum(query_heads * key_heads, axis=-1) * (1.0 / math.sqrt(head_size))
    top_all = jnp.maximum(part_top, own_score)
    keep_factor = jnp.exp(part_top - top_all)
    own_weight = jnp.exp(own_score - top_all)
    total_all = part_sum * keep_factor + own_weight
    summed = (
        part_out.reshape(request_count, heads_local, head_size) * keep_factor[..., None]
        + own_weight[..., None] * value_heads
    )
    attention = (
        (summed / total_all[..., None]).astype(jnp.bfloat16).reshape(request_count, feat_width)
    )
    log_sum_exp = top_all + jnp.log(total_all)
    write_rows = jnp.concatenate(
        [
            jnp.where(remote, cache_rows, my_start + my_length),
            jnp.where(in_live, in_start + in_length, cache_rows),
        ]
    )
    write_keys = jnp.concatenate([keys_new, arrived[:, feat_width : 2 * feat_width]], axis=0)
    write_values = jnp.concatenate([values_new, arrived[:, 2 * feat_width :]], axis=0)
    kv_updated = kv_cache.at[0, write_rows].set(write_keys, mode="drop")
    kv_updated = kv_updated.at[1, write_rows].set(write_values, mode="drop")
    attn_mine = lax.psum_scatter(
        jnp.dot(attention, project_out, preferred_element_type=jnp.float32),
        "tensor",
        scatter_dimension=0,
        tiled=True,
    )
    resid = (tokens.astype(jnp.float32) + attn_mine).astype(jnp.bfloat16)
    inner = expand_hidden(
        lax.all_gather(scaled_norm(resid, mlp_gain), "tensor", axis=0, tiled=True), gate_up
    )
    down_mine = lax.psum_scatter(
        jnp.dot(inner, project_down, preferred_element_type=jnp.float32),
        "tensor",
        scatter_dimension=0,
        tiled=True,
    )
    hidden_states = (resid.astype(jnp.float32) + down_mine).astype(jnp.bfloat16)
    return (hidden_states, log_sum_exp, kv_updated)


def solution(mesh):
    placed = (
        P(("dp", "tensor"), None),
        P(),
        P(),
        P(None, None, "tensor"),
        P("tensor", None),
        P(None, None, "tensor"),
        P("tensor", None),
        P(None, "dp", "tensor"),
        P(),
        P(),
        P(),
    )
    return jax.shard_map(
        on_device,
        mesh=mesh,
        in_specs=placed,
        out_specs=(P(("dp", "tensor"), None), P("dp", "tensor"), P(None, "dp", "tensor")),
        check_vma=False,
    )
```

profile of v0, /device:TPU:32, one launch (start us, length us, event | category | flops | bytes accessed | tf_op | source)
XLA Modules:
  0.0 343.5 jit_solution(1785069862997310190)
XLA Ops:
  7.3 3.2 copy.216
  12.1 0.7 add_select_fusion.1
  14.3 2.7 copy.170
  18.5 32.8 %all-gather.3.cloned.1.call-done = bf16[256,2048]{1,0:T(8,128)(2,1)} async-done(((bf16[16,2048]{1,0:T(8,128)(2,1)}), bf16[256,2048]{1,0:T(8,128)(2,1)}) %all-gather.3.cloned.1.call-update) | async-done | bytes 1048592 | tf_op jit(solution)/shard_map/all_gather | solution.py:108
  51.3 1.5 fusion.8
  52.8 2.4 fusion.11
  55.4 0.6 multiply_reduce_fusion
  56.0 0.6 copy-done.5
  56.8 0.7 reshape.405
  57.5 6.8 %all-to-all-start = ((bf16[16,9,384]{2,1,0:T(8,128)(2,1)}), bf16[16,9,384]{2,1,0:T(8,128)(2,1)S(1)}, u32[]{:S(2)}, u32[]{:S(2)}) async-start(bf16[16,9,384]{2,1,0:T(8,128)(2,1)} %reshape.405), calls=%async_computation | async-start | bytes 393216 | tf_op jit(solution)/shard_map/all_to_all | solution.py:134
  64.4 0.7 fusion.45
  65.7 7.0 %all-to-all-done = bf16[16,9,384]{2,1,0:T(8,128)(2,1)S(1)} async-done(((bf16[16,9,384]{2,1,0:T(8,128)(2,1)}), bf16[16,9,384]{2,1,0:T(8,128)(2,1)S(1)}, u32[]{:S(2)}, u32[]{:S(2)}) %all-to-all-start) | async-done | bytes 110624 | tf_op jit(solution)/shard_map/all_to_all | solution.py:134
  72.7 0.6 fusion.51
  73.5 29.1 %while.14 = (s32[]{:T(128)}, f32[400,2]{0,1:T(2,128)S(1)}, f32[400,2]{0,1:T(2,128)S(1)}, f32[400,2,64]{0,2,1:T(8,128)S(1)}, s32[]{:T(128)}, /*index=5*/s32[400]{...) while((s32[]{:T(128)}, f32[400,2]{0,1:T(2,128)S(1)}, ...), condition=%wide.region_13.14_spmd, body=%wide.region_10.13_spmd.sunk | while | flops 370997312 | bytes 7615819 | solution.py:81
  73.8 1.0 constant_dynamic-slice_fusion.3
  75.0 0.6 fusion.70
  75.7 0.6 fusion.71
  76.3 1.4 fusion.72
  77.9 1.0 constant_dynamic-slice_fusion.3
  79.2 0.6 fusion.70
  79.8 0.6 fusion.71
  80.4 1.4 fusion.72
  82.1 1.0 constant_dynamic-slice_fusion.3
  83.3 0.6 fusion.70
  84.0 0.6 fusion.71
  84.6 1.4 fusion.72
  86.2 1.0 constant_dynamic-slice_fusion.3
  87.5 0.6 fusion.70
  88.1 0.6 fusion.71
  88.7 1.4 fusion.72
  90.4 1.0 constant_dynamic-slice_fusion.3
  91.6 0.6 fusion.70
  92.3 0.6 fusion.71
  92.9 1.4 fusion.72
  94.5 1.0 constant_dynamic-slice_fusion.3
  95.8 0.6 fusion.70
  97.0 1.4 fusion.72
  98.7 1.0 constant_dynamic-slice_fusion.3
  99.9 0.6 fusion.70
  101.2 1.4 fusion.72
  102.7 0.6 copy.179
  103.3 7.4 %all-to-all-start.3 = ((f32[16,9,2]{1,2,0:T(2,128)}), f32[16,9,2]{1,2,0:T(2,128)S(1)}, u32[]{:S(2)}, u32[]{:S(2)}) async-start(f32[16,9,2]{1,2,0:T(2,128)} %copy.179), calls=%async_computation.3 | async-start | bytes 32768 | tf_op jit(solution)/shard_map/all_to_all | solution.py:177
  110.9 0.6 copy.175
  111.5 6.9 %all-to-all-done.3 = f32[16,9,2]{1,2,0:T(2,128)S(1)} async-done(((f32[16,9,2]{1,2,0:T(2,128)}), f32[16,9,2]{1,2,0:T(2,128)S(1)}, u32[]{:S(2)}, u32[]{:S(2)}) %all-to-all-start.3) | async-done | bytes 1184 | tf_op jit(solution)/shard_map/all_to_all | solution.py:177
  118.3 3.5 %all-to-all-start.2 = ((f32[16,9,2]{1,2,0:T(2,128)}), f32[16,9,2]{1,2,0:T(2,128)S(1)}, u32[]{:S(2)}, u32[]{:S(2)}) async-start(f32[16,9,2]{1,2,0:T(2,128)} %copy.175), calls=%async_computation.2 | async-start | bytes 32768 | tf_op jit(solution)/shard_map/all_to_all | solution.py:170
  122.0 0.8 reshape.407
  122.9 6.5 %all-to-all-done.2 = f32[16,9,2]{1,2,0:T(2,128)S(1)} async-done(((f32[16,9,2]{1,2,0:T(2,128)}), f32[16,9,2]{1,2,0:T(2,128)S(1)}, u32[]{:S(2)}, u32[]{:S(2)}) %all-to-all-start.2) | async-done | bytes 1184 | tf_op jit(solution)/shard_map/all_to_all | solution.py:170
  129.4 3.5 %all-to-all-start.1 = ((f32[16,9,128]{2,1,0:T(8,128)}), f32[16,9,128]{2,1,0:T(8,128)S(1)}, u32[]{:S(2)}, u32[]{:S(2)}) async-start(f32[16,9,128]{2,1,0:T(8,128)} %reshape.407), calls=%async_computation.1 | async-start | bytes 262144 | tf_op jit(solution)/shard_map/all_to_all | solution.py:163
  133.2 0.7 gather_fusion.1
  134.1 0.9 gather_fusion.2
  135.1 1.3 log_add_fusion
  136.4 4.3 %all-to-all-done.1 = f32[16,9,128]{2,1,0:T(8,128)S(1)} async-done(((f32[16,9,128]{2,1,0:T(8,128)}), f32[16,9,128]{2,1,0:T(8,128)S(1)}, u32[]{:S(2)}, u32[]{:S(2)}) %all-to-all-start.1) | async-done | bytes 73760 | tf_op jit(solution)/shard_map/all_to_all | solution.py:163
  140.7 0.9 gather_fusion
  141.8 1.8 fusion.52
  143.7 52.3 %reduce-scatter.3.cloned.1.call-done = f32[16,2048]{1,0:T(8,128)} async-done(((f32[256,2048]{1,0:T(8,128)}), f32[16,2048]{1,0:T(8,128)}) %reduce-scatter.3.cloned.1.call-update) | async-done | bytes 131088 | tf_op jit(solution)/shard_map/reduce_scatter | solution.py:227
  195.9 1.0 fusion.29
  197.0 0.7 fusion.31
  197.9 39.9 %all-gather.5.cloned.1.call-done = bf16[256,2048]{1,0:T(8,128)(2,1)} async-done(((bf16[16,2048]{1,0:T(8,128)(2,1)}), bf16[256,2048]{1,0:T(8,128)(2,1)}) %all-gather.5.cloned.1.call-update) | async-done | bytes 1048592 | tf_op jit(solution)/shard_map/all_gather | solution.py:235
  237.9 3.7 %fusion.13 = f32[256,2,512]{2,0,1:T(8,128)S(1)} fusion(bf16[2,2048,512]{2,1,0:T(8,128)(2,1)} %param.20, bf16[256,2048]{1,0:T(8,128)(2,1)} %all-gather.5.cloned.1.call-done), kind=kOutput, calls=%fused_computation.28 | convolution fusion | flops 1073741824 | bytes 6291456 | tf_op jit(solution)/shard_map/rd,cdf->rcf/dot_general | solution.py:37
  241.6 2.1 fusion.19
  243.8 0.6 copy-done.18
  245.1 45.2 %scatter_fusion = bf16[2,4096,128]{2,1,0:T(8,128)(2,1)} fusion(bf16[2,4096,128]{2,1,0:T(8,128)(2,1)} %get-tuple-element.316, s32[400]{0:T(512)S(1)} %bitcast.99, bf16[400,128]{1,0:T(8,128)(2,1)S(1)} %copy.184), kind=kCustom, calls=%fused_computation.3 | custom fusion | bytes 310400 | tf_op jit(solution)/shard_map/scatter | solution.py:225
  290.3 45.1 %scatter_fusion.1 = bf16[2,4096,128]{2,1,0:T(8,128)(2,1)} fusion(bf16[2,4096,128]{2,1,0:T(8,128)(2,1)} %scatter_fusion, s32[400]{0:T(512)S(1)} %bitcast.98, bf16[400,128]{1,0:T(8,128)(2,1)S(1)} %copy.186), kind=kCustom, calls=%fused_computation.4 | custom fusion | bytes 310400 | tf_op jit(solution)/shard_map/scatter | solution.py:226
  335.4 1.6 fusion.32
  (172 shorter events, 11.8 us)
Async XLA Ops:
  7.2 234.5 %copy-start = (bf16[512,2048]{1,0:T(8,128)(2,1)S(1)}, bf16[512,2048]{1,0:T(8,128)(2,1)}, u32[]{:S(2)}) copy-start(bf16[512,2048]{1,0:T(8,128)(2,1)} %param.21) | copy-start | bytes 6291460
  7.2 4.8 %copy-start.16 = (bf16[2048]{0:T(1024)(128)(2,1)S(1)}, bf16[2048]{0:T(1024)(128)(2,1)}, u32[]{:S(2)}) copy-start(bf16[2048]{0:T(1024)(128)(2,1)} %param.16) | copy-start | bytes 12292
  7.2 4.9 %copy-start.11 = (s32[4096]{0:T(1024)S(1)}, s32[4096]{0:T(1024)}, u32[]{:S(2)}) copy-start(s32[4096]{0:T(1024)} %param.23) | copy-start | bytes 49156
  7.2 3.3 copy-start.12
  7.2 4.8 %copy-start.13 = (s32[4096]{0:T(1024)S(1)}, s32[4096]{0:T(1024)}, u32[]{:S(2)}) copy-start(s32[4096]{0:T(1024)} %param.25) | copy-start | bytes 49156
  7.2 44.1 %all-gather.3.cloned.1.call-start = ((), (), s32[]{:S(2)}) async-start(), calls=%async_computation.6 | async-start | bytes 1114112 | tf_op jit(solution)/shard_map/all_gather | solution.py:108
  12.7 40.1 %copy-start.9 = (pred[256]{0:T(512)(128)(4,1)}, pred[256]{0:T(512)(128)(4,1)S(1)}, u32[]{:S(2)}) copy-start(pred[256]{0:T(512)(128)(4,1)S(1)} %get-tuple-element.163) | copy-start | bytes 772
  55.3 0.7 copy-start.3
  56.0 0.6 copy-start.5
  57.5 15.1 %all-to-all-start = ((bf16[16,9,384]{2,1,0:T(8,128)(2,1)}), bf16[16,9,384]{2,1,0:T(8,128)(2,1)S(1)}, u32[]{:S(2)}, u32[]{:S(2)}) async-start(bf16[16,9,384]{2,1,0:T(8,128)(2,1)} %reshape.405), calls=%async_computation | async-start | bytes 393216 | tf_op jit(solution)/shard_map/all_to_all | solution.py:134
  103.3 15.0 %all-to-all-start.3 = ((f32[16,9,2]{1,2,0:T(2,128)}), f32[16,9,2]{1,2,0:T(2,128)S(1)}, u32[]{:S(2)}, u32[]{:S(2)}) async-start(f32[16,9,2]{1,2,0:T(2,128)} %copy.179), calls=%async_computation.3 | async-start | bytes 32768 | tf_op jit(solution)/shard_map/all_to_all | solution.py:177
  118.3 11.0 %all-to-all-start.2 = ((f32[16,9,2]{1,2,0:T(2,128)}), f32[16,9,2]{1,2,0:T(2,128)S(1)}, u32[]{:S(2)}, u32[]{:S(2)}) async-start(f32[16,9,2]{1,2,0:T(2,128)} %copy.175), calls=%async_computation.2 | async-start | bytes 32768 | tf_op jit(solution)/shard_map/all_to_all | solution.py:170
  121.9 11.3 %copy-start.14 = (s32[1024]{0:T(1024)}, s32[1024]{0:T(1024)S(1)}, u32[]{:S(2)}) copy-start(s32[1024]{0:T(1024)S(1)} %pad_clamp_fusion) | copy-start | bytes 12292
  129.4 11.3 %all-to-all-start.1 = ((f32[16,9,128]{2,1,0:T(8,128)}), f32[16,9,128]{2,1,0:T(8,128)S(1)}, u32[]{:S(2)}, u32[]{:S(2)}) async-start(f32[16,9,128]{2,1,0:T(8,128)} %reshape.407), calls=%async_computation.1 | async-start | bytes 262144 | tf_op jit(solution)/shard_map/all_to_all | solution.py:163
  132.9 63.0 %reduce-scatter.3.cloned.1.call-start = ((), (), s32[]{:S(2)}) async-start(), calls=%async_computation.7 | async-start | bytes 2228224 | tf_op jit(solution)/shard_map/reduce_scatter | solution.py:227
  133.2 8.5 %copy-start.10 = (pred[256]{0:T(512)(128)(4,1)S(1)}, pred[256]{0:T(512)(128)(4,1)}, u32[]{:S(2)}) copy-start(pred[256]{0:T(512)(128)(4,1)} %copy-done.9) | copy-start | bytes 772
  133.2 8.5 %copy-start.15 = (pred[256]{0:T(512)(128)(4,1)S(1)}, pred[256]{0:T(512)(128)(4,1)}, u32[]{:S(2)}) copy-start(pred[256]{0:T(512)(128)(4,1)} %get-tuple-element.171) | copy-start | bytes 772
  133.9 7.8 %copy-start.1 = (bf16[128,2048]{1,0:T(8,128)(2,1)S(1)}, bf16[128,2048]{1,0:T(8,128)(2,1)}, u32[]{:S(2)}) copy-start(bf16[128,2048]{1,0:T(8,128)(2,1)} %param.19) | copy-start | bytes 1572868
  141.7 1.9 copy-start.17
  141.7 54.2 %copy-start.2 = (bf16[16,2048]{1,0:T(8,128)(2,1)S(1)}, bf16[16,2048]{1,0:T(8,128)(2,1)}, u32[]{:S(2)}) copy-start(bf16[16,2048]{1,0:T(8,128)(2,1)} %param.15) | copy-start | bytes 196612
  143.6 94.3 %all-gather.5.cloned.1.call-start = ((), (), s32[]{:S(2)}) async-start(), calls=%async_computation.8 | async-start | bytes 1114112 | tf_op jit(solution)/shard_map/all_gather | solution.py:235
  197.7 137.7 %reduce-scatter.5.cloned.1.call-start = ((), (), s32[]{:S(2)}) async-start(), calls=%async_computation.9 | async-start | bytes 2228224 | tf_op jit(solution)/shard_map/reduce_scatter | solution.py:237
  243.8 0.7 copy-start.18
  243.8 0.7 copy-start.19
  243.8 0.8 copy-start.8
  243.8 0.9 copy-start.4
  243.8 1.0 copy-start.7
  243.8 1.1 copy-start.6
Sparse Core Ops, SparseCore 0:
  10.6 40.6 all-gather.2
  143.7 52.1 reduce-scatter.2
  198.3 39.5 all-gather.4
  243.9 55.3 reduce-scatter.4
where the time goes:
time: 348 us; the launch traced here: 344 us
  waiting for transfers between devices  150 us (43%)
  local copies, waits for them, and re-layouts  115 us (33%)
  matrix products  24.2 us (7%)
  starting transfers between devices  21.6 us (6%)
  other arithmetic  17.9 us (5%)
  between operations  15 us (4%)
    reduce_scatter x1, waiting for transfers between devices, on_device(): lax.psum_scatter(jnp.dot(attention, project_out, preferred_element_type=j...  52.3 us
    scatter x1, local copies, waits for them, and re-layouts, on_device(): kv_updated = kv_cache.at[0, write_rows].set(write_keys, mode='drop')  45.2 us
    scatter x1, local copies, waits for them, and re-layouts, on_device(): kv_updated = kv_updated.at[1, write_rows].set(write_values, mode='drop')  45.1 us
    all_gather x1, waiting for transfers between devices, on_device(): lax.all_gather(scaled_norm(resid, mlp_gain), 'tensor', axis=0, tiled=True)  39.9 us
    all_gather x1, waiting for transfers between devices, on_device(): gathered = lax.all_gather(tokens, 'tensor', axis=0, tiled=True)  32.8 us
    dot_general x7, matrix products, advance(): jnp.einsum('qhp,phe->qhe', weights, value_block, precision=lax.Precision....  9.6 us
    all_to_all x1, starting transfers between devices, on_device(): lax.all_to_all(far_sum.reshape(groups, capacity, heads_local), 'dp', spli...  7.44 us
    unnamed x44, local copies, waits for them, and re-layouts  7.43 us
  transfers between devices with their start and end apart: 8, of which 7 were waited for; matrix products, arithmetic and copies ran while one was open for 30% of the time, Pallas kernels for 0%

commit v1 on v0

v1 whole, which is shorter than its diff:
```python
import functools

import jax
import jax.numpy as jnp
import numpy as np
from jax import lax
from jax.experimental import pallas as pl
from jax.experimental.pallas import tpu as pltpu
from jax.sharding import PartitionSpec as P

MESH = pl.DeviceIdType.MESH
BF = jnp.bfloat16
F32 = jnp.float32
I32 = jnp.int32

EPS = 1e-05
ROPE_BASE = 130000.0
LOW = -1e30
HD = 64
NDP = 16
NTP = 16
NZ = 8
D = 2048
HALF = 1024
BLK = 16
REQ = 256
HOME = 128
SLOTS = HOME + NDP * BLK
ROWS = 4096
FFL = 512
PBLK = 512

AG_RIGHT = ((1, 0), (1, 1), (2, 0), (2, 1), (3, 0), (3, 1), (4, 0))
AG_LEFT = ((1, 1), (1, 0), (2, 1), (2, 0), (3, 1), (3, 0), (4, 1))
RS_RIGHT = ((4, 0), (3, 1), (3, 0), (2, 1), (2, 0), (1, 1), (1, 0))
RS_LEFT = ((4, 1), (3, 0), (3, 1), (2, 0), (2, 1), (1, 0), (1, 1))


class Place:
    def __init__(self):
        self.d = lax.axis_index("dp")
        self.t = lax.axis_index("tensor")
        self.z = self.t // 2
        self.c = self.t % 2
        self.sib = (self.d, self.t + 1 - 2 * self.c)
        self.zdev = (
            (self.d, ((self.z + 1) % NZ) * 2 + self.c),
            (self.d, ((self.z + NZ - 1) % NZ) * 2 + self.c),
        )

    def dp_peer(self, offset):
        return (self.d + offset) % NDP


def greet(me):
    barrier = pltpu.get_barrier_semaphore()
    targets = [me.zdev[0], me.zdev[1], me.sib]
    targets += [(me.dp_peer(i), me.t) for i in range(1, NDP)]
    for target in targets:
        pl.semaphore_signal(barrier, inc=1, device_id=target, device_id_type=MESH)
    return lambda: pl.semaphore_wait(barrier, len(targets))


def iota(shape, axis):
    return lax.broadcasted_iota(I32, shape, axis)


def scaled_norm(wide, gain):
    factor = lax.rsqrt(jnp.mean(wide * wide, axis=-1, keepdims=True) + EPS)
    return (wide * factor * gain).astype(BF)


def all_gather_z(me, buf, row_of, ring_send, ring_recv, sib_send, sib_recv):
    lists = (AG_RIGHT, AG_LEFT)
    signs = (1, -1)
    sib_copies = []
    started = []

    def block(origin, half):
        return buf.at[half, pl.ds(pl.multiple_of(row_of(origin, me.c), BLK), BLK), :]

    def message(way, index):
        k, half = lists[way][index]
        origin = (me.z + NZ - signs[way] * (k - 1)) % NZ
        ref = block(origin, half)
        return pltpu.make_async_remote_copy(
            src_ref=ref, dst_ref=ref, send_sem=ring_send.at[way, index], recv_sem=ring_recv.at[way, index],
            device_id=me.zdev[way], device_id_type=MESH,
        )

    def sibling(origin, half):
        index = len(sib_copies)
        ref = block(origin, half)
        copy = pltpu.make_async_remote_copy(
            src_ref=ref, dst_ref=ref, send_sem=sib_send.at[index], recv_sem=sib_recv.at[index],
            device_id=me.sib, device_id_type=MESH,
        )
        copy.start()
        sib_copies.append(copy)

    def start(way, index):
        copy = message(way, index)
        copy.start()
        started.append(copy)

    def begin():
        for index in range(2):
            for way in range(2):
                start(way, index)
        for half in range(2):
            sibling(me.z, half)

    def finish():
        for index in range(7):
            for way in range(2):
                k, half = lists[way][index]
                message(way, index).wait_recv()
                if (k + 1, half) in lists[way]:
                    start(way, lists[way].index((k + 1, half)))
                sibling((me.z + NZ - signs[way] * k) % NZ, half)
        for copy in sib_copies:
            copy.wait_recv()

    def drain():
        for copy in started:
            copy.wait_send()
        for copy in sib_copies:
            copy.wait_send()

    return begin, finish, drain


def reduce_scatter_z(me, product, sib_out, sib_in, own, ring_out, ring_in, ring_send, ring_recv, sib_send, sib_recv):
    lists = (RS_RIGHT, RS_LEFT)
    signs = (1, -1)
    started = []

    def message(way, index):
        return pltpu.make_async_remote_copy(
            src_ref=ring_out.at[way, index], dst_ref=ring_in.at[way, index],
            send_sem=ring_send.at[way, index], recv_sem=ring_recv.at[way, index],
            device_id=me.zdev[way], device_id_type=MESH,
        )

    def mine(way, distance, half):
        target = (me.z + NZ + signs[way] * distance) % NZ
        return own[half, pl.ds(pl.multiple_of(target * BLK, BLK), BLK), :]

    def send(way, index, value):
        ring_out[way, index] = value.astype(BF)
        copy = message(way, index)
        copy.start()
        started.append(copy)

    for half in range(2):
        product(half, 1 - me.c, sib_out)
        copy = pltpu.make_async_remote_copy(
            src_ref=sib_out.at[half], dst_ref=sib_in.at[half], send_sem=sib_send.at[half], recv_sem=sib_recv.at[half],
            device_id=me.sib, device_id_type=MESH,
        )
        copy.start()
        started.append(copy)
        product(half, me.c, own)
    for half in range(2):
        started[half].wait_recv()
        own[half] = own[half] + sib_in[half].astype(F32)
        first = half
        send(first, 0, mine(first, 4, half))
        send(1 - first, 1, mine(1 - first, 3, half))
        if half == 1:
            pass
    total = [own[half, pl.ds(pl.multiple_of(me.z * BLK, BLK), BLK), :] for half in range(2)]
    for index in range(7):
        for way in range(2):
            distance, half = lists[way][index]
            message(way, index).wait_recv()
            arrived = ring_in[way, index].astype(F32)
            if distance > 1:
                send(way, lists[way].index((distance - 1, half)), arrived + mine(way, distance - 1, half))
            else:
                total[half] = total[half] + arrived
    return total, lambda: [copy.wait_send() for copy in started]


def exchange_dp(me, source, landing, send, recv):
    copies = []
    for i in range(1, NDP):
        peer = me.dp_peer(i)
        copy = pltpu.make_async_remote_copy(
            src_ref=source.at[pl.ds(pl.multiple_of(peer * BLK, BLK), BLK), :],
            dst_ref=landing.at[pl.ds(pl.multiple_of(me.d * BLK, BLK), BLK), :],
            send_sem=send.at[i - 1], recv_sem=recv.at[i - 1],
            device_id=(peer, me.t), device_id_type=MESH,
        )
        copy.start()
        copies.append(copy)
    here = pl.ds(pl.multiple_of(me.d * BLK, BLK), BLK)
    landing[here, :] = source[here, :]
    return copies


def column_of(row, hits):
    return jnp.sum(jnp.where(hits, row, 0.0), axis=1, keepdims=True)


def first_kernel(
    tokens, gain, lengths, owners, starts, freqs, w_hbm,
    compact_out, start_out, end_out, end_row_out, sel_out, scat_out,
    gathered, w, packed, outgoing, arrived,
    ring_send, ring_recv, sib_send, sib_recv, dp_send, dp_recv, w_sem,
):
    me = Place()
    w_copies = [
        pltpu.make_async_copy(w_hbm.at[m], w.at[:, pl.ds(m * 128, 128)], w_sem.at[m]) for m in range(3)
    ]
    for copy in w_copies:
        copy.start()
    wait_all = greet(me)
    normed = scaled_norm(tokens[...].astype(F32), gain[...].astype(F32))
    row_of = lambda zz, cc: (zz * 2 + cc) * BLK
    my_rows = pl.ds(pl.multiple_of(row_of(me.z, me.c), BLK), BLK)
    for half in range(2):
        gathered[half, my_rows, :] = normed[:, half * HALF : (half + 1) * HALF]
    wait_all()
    begin, finish, drain = all_gather_z(me, gathered, row_of, ring_send, ring_recv, sib_send, sib_recv)
    begin()

    def wide(ref):
        return jnp.concatenate([ref[pl.ds(0, NDP, stride=2), :], ref[pl.ds(1, NDP, stride=2), :]], axis=1)

    def mine(ref):
        return jnp.concatenate([ref[pl.ds(2 * me.d, 1), :], ref[pl.ds(2 * me.d + 1, 1), :]], axis=1)

    own_all, len_all, start_all = wide(owners), wide(lengths), wide(starts)
    own_row, len_row, start_row = mine(owners), mine(lengths).astype(F32), mine(starts).astype(F32)
    before = jnp.where(iota((REQ, REQ), 0) < iota((REQ, REQ), 1), 1.0, 0.0).astype(BF)
    here = own_all == me.d
    here_rank = jnp.dot(jnp.where(here, 1.0, 0.0).astype(BF), before, preferred_element_type=F32)
    away = here & (iota((NDP, REQ), 0) != me.d)
    place_in = jnp.where(away, here_rank, -1.0)
    onehot = jnp.where(iota((NDP, REQ), 0) == own_row, 1.0, 0.0)
    counts = jnp.dot(onehot.astype(BF), before, preferred_element_type=F32)
    rank = jnp.sum(onehot * counts, axis=0, keepdims=True)
    own_wide = own_row.astype(F32)
    place = jnp.where(own_row == me.d, rank, HOME + own_wide * BLK + rank)
    sel = iota((SLOTS, REQ), 0).astype(F32) == place
    sel_out[...] = jnp.where(sel, 1.0, 0.0).astype(BF)
    request = iota((REQ, REQ), 0)
    natural = ((request >> 4) & 7) * 32 + (request >> 7) * 16 + (request & 15)
    place_col = column_of(place, natural == iota((REQ, REQ), 1))
    scat_out[...] = jnp.where(iota((REQ, SLOTS), 1).astype(F32) == place_col, 1.0, 0.0).astype(BF)

    def spread(rows16):
        return jnp.concatenate(
            [jnp.broadcast_to(rows16[b : b + 1, :], (BLK, REQ)) for b in range(NDP)], axis=0
        )

    slot = (iota((NDP * BLK, REQ), 0) & (BLK - 1)).astype(F32)
    hits_in = spread(place_in) == slot
    begin_all = start_all.astype(F32)
    finish_all = begin_all + len_all.astype(F32)
    hits_home = sel[:HOME]
    begin_col = jnp.concatenate(
        [column_of(start_row + 1.0, hits_home), column_of(spread(begin_all) + 1.0, hits_in)], axis=0
    ) - 1.0
    finish_col = jnp.concatenate(
        [column_of(start_row + len_row + 1.0, hits_home), column_of(spread(finish_all) + 1.0, hits_in)], axis=0
    ) - 1.0
    start_out[...] = jnp.broadcast_to(begin_col, (SLOTS, 128))
    end_out[...] = jnp.broadcast_to(finish_col, (SLOTS, 128))
    eye = iota((SLOTS, SLOTS), 0) == iota((SLOTS, SLOTS), 1)
    end_row = jnp.sum(jnp.where(eye, finish_col, 0.0), axis=0, keepdims=True)
    end_row_out[...] = jnp.broadcast_to(end_row, (8, SLOTS))

    len_col = column_of(len_row, iota((REQ, REQ), 0) == iota((REQ, REQ), 1))
    angle = len_col * freqs[...]
    turns = jnp.floor(angle * (1.0 / (2.0 * np.pi)) + 0.5)
    left = (angle - turns * 6.28125) - turns * np.float32(2.0 * np.pi - 6.28125)
    x = 0.5 * left
    x2 = x * x
    sin_half = x * (1.0 + x2 * (-1 / 6 + x2 * (1 / 120 + x2 * (-1 / 5040 + x2 * (1 / 362880 - x2 / 39916800)))))
    cos_half = 1.0 + x2 * (
        -1 / 2 + x2 * (1 / 24 + x2 * (-1 / 720 + x2 * (1 / 40320 + x2 * (-1 / 3628800 + x2 / 479001600))))
    )
    sine = 2.0 * sin_half * cos_half
    cosine = 1.0 - 2.0 * sin_half * sin_half
    low_half = (iota((REQ, 128), 1) & (HD - 1)) < HD // 2
    signed = jnp.where(low_half, -sine, sine)

    finish()
    for copy in w_copies:
        copy.wait()
    projected = jnp.dot(gathered[0], w[:HALF], preferred_element_type=F32)
    projected = projected + jnp.dot(gathered[1], w[HALF:], preferred_element_type=F32)

    def turned(values):
        partner = jnp.where(low_half, pltpu.roll(values, 96, 1), pltpu.roll(values, 32, 1))
        return (values * cosine + partner * signed).astype(BF)

    packed[:, 0:128] = turned(projected[:, 0:128])
    packed[:, 128:256] = turned(projected[:, 128:256])
    packed[:, 256:384] = projected[:, 256:384].astype(BF)
    compact = jnp.dot(sel_out[...], packed[...], preferred_element_type=F32).astype(BF)
    outgoing[...] = compact[HOME:]
    copies = exchange_dp(me, outgoing, arrived, dp_send, dp_recv)
    compact_out[:HOME, :] = compact[:HOME]
    drain()
    for copy in copies:
        copy.wait_recv()
    compact_out[HOME:, :] = arrived[...]
    for copy in copies:
        copy.wait_send()


def middle_kernel(compact, start_ref, end_ref, end_row, cache, cache_out, ret, q2, live_top, live_sum, live_out):
    step = pl.program_id(0)
    low_lanes = iota((SLOTS, 128), 1) < HD

    @pl.when(step == 0)
    def _():
        q = compact[:, 0:128].astype(F32) * (1.0 / 8.0)
        k = compact[:, 128:256].astype(F32)
        v = compact[:, 256:384].astype(F32)
        for head in range(2):
            keep = low_lanes if head == 0 else jnp.logical_not(low_lanes)
            qh = jnp.where(keep, q, 0.0)
            rows = pl.ds(head * SLOTS, SLOTS)
            q2[rows, :] = qh.astype(BF)
            live_top[rows, :] = jnp.broadcast_to(jnp.sum(qh * k, axis=1, keepdims=True), (SLOTS, 128))
            live_sum[rows, :] = jnp.ones((SLOTS, 128), F32)
            live_out[rows, :] = v

    keys = cache[0]
    values = cache[1]
    base = step * PBLK
    position = (iota((PBLK, SLOTS), 0) + base).astype(F32)
    place = jnp.where(position == end_row[0:1, :], 1.0, 0.0)
    hit = jnp.max(place, axis=1, keepdims=True) > 0.5
    fresh = jnp.dot(place.astype(BF), compact[:, 128:384], preferred_element_type=F32)
    cache_out[0] = jnp.where(hit, fresh[:, 0:128], keys.astype(F32)).astype(BF)
    cache_out[1] = jnp.where(hit, fresh[:, 128:256], values.astype(F32)).astype(BF)

    across = (iota((SLOTS, PBLK), 1) + base).astype(F32)
    live = (across >= start_ref[:, 0:1]) & (across < end_ref[:, 0:1])
    for head in range(2):
        rows = pl.ds(head * SLOTS, SLOTS)
        scores = lax.dot_general(q2[rows, :], keys, (((1,), (1,)), ((), ())), preferred_element_type=F32)
        scores = jnp.where(live, scores, LOW)
        old_top = live_top[rows, 0:1]
        top = jnp.maximum(old_top, jnp.max(scores, axis=1, keepdims=True))
        weights = jnp.where(live, jnp.exp(scores - top), 0.0)
        factor = jnp.exp(old_top - top)
        live_sum[rows, :] = live_sum[rows, :] * factor + jnp.sum(weights, axis=1, keepdims=True)
        live_out[rows, :] = live_out[rows, :] * factor + jnp.dot(weights.astype(BF), values, preferred_element_type=F32)
        live_top[rows, :] = jnp.broadcast_to(top, (SLOTS, 128))

    @pl.when(step == pl.num_programs(0) - 1)
    def _():
        out = live_out[...] / live_sum[...]
        ret[:, 0:128] = jnp.where(low_lanes, out[:SLOTS], out[SLOTS:]).astype(BF)
        lse = live_top[...] + jnp.log(live_sum[...])
        high = lse.astype(BF).astype(F32)
        low = lse - high
        lane = iota((SLOTS, 128), 1)
        tail = jnp.where(lane == 0, high[:SLOTS], jnp.where(lane == 1, low[:SLOTS], jnp.where(lane == 2, high[SLOTS:], low[SLOTS:])))
        ret[:, 128:256] = tail.astype(BF)


def last_kernel(
    tokens, gain, ret, sel, scat, wo_hbm, gu_hbm, wd_hbm,
    hidden_out, lse_out,
    slots, landing, outgoing, attended, wo, gu, wd, gathered, inner, resid_keep,
    sib_out, sib_in, own, ring_out, ring_in,
    dp_send, dp_recv, ag_ring_send, ag_ring_recv, ag_sib_send, ag_sib_recv,
    rs_ring_send, rs_ring_recv, rs_sib_send, rs_sib_recv, w_sem,
):
    me = Place()
    wait_all = greet(me)
    w_copies = [
        pltpu.make_async_copy(wo_hbm, wo, w_sem.at[0]),
        pltpu.make_async_copy(gu_hbm, gu, w_sem.at[1]),
        pltpu.make_async_copy(wd_hbm, wd, w_sem.at[2]),
    ]
    for copy in w_copies:
        copy.start()
    outgoing[...] = ret[HOME:, :]
    slots[:HOME, :] = ret[:HOME, :]
    wait_all()
    copies = exchange_dp(me, outgoing, landing, dp_send, dp_recv)
    for copy in copies:
        copy.wait_recv()
    slots[HOME:, :] = landing[...]
    attended[...] = jnp.dot(scat[...], slots[:, 0:128], preferred_element_type=F32).astype(BF)
    w_copies[0].wait()

    def out_product(half, core, target):
        rows = pl.ds(pl.multiple_of(core * 128, 128), 128)
        value = jnp.dot(attended[rows, :], wo[:, half * HALF : (half + 1) * HALF], preferred_element_type=F32)
        target[half] = value.astype(target.dtype)

    total, drain_first = reduce_scatter_z(
        me, out_product, sib_out.at[0], sib_in.at[0], own, ring_out.at[0], ring_in.at[0],
        rs_ring_send.at[0], rs_ring_recv.at[0], rs_sib_send.at[0], rs_sib_recv.at[0],
    )
    resid = tokens[...].astype(F32) + jnp.concatenate(total, axis=1)
    resid = resid.astype(BF)
    resid_keep[...] = resid
    normed = scaled_norm(resid.astype(F32), gain[...].astype(F32))
    row_of = lambda zz, cc: cc * 128 + zz * BLK
    my_rows = pl.ds(pl.multiple_of(row_of(me.z, me.c), BLK), BLK)
    for half in range(2):
        gathered[half, my_rows, :] = normed[:, half * HALF : (half + 1) * HALF]
    begin, finish, drain = all_gather_z(me, gathered, row_of, ag_ring_send, ag_ring_recv, ag_sib_send, ag_sib_recv)
    begin()
    wide = sel[...].astype(F32)
    tail = slots[:, 128:256].astype(F32)
    for head in range(2):
        lse = tail[:, 2 * head : 2 * head + 1] + tail[:, 2 * head + 1 : 2 * head + 2]
        lse_out[head : head + 1, :] = jnp.sum(wide * lse, axis=0, keepdims=True)
    drain_first()
    for copy in copies:
        copy.wait_send()
    finish()
    w_copies[1].wait()
    w_copies[2].wait()
    for tile in range(FFL // 256):
        columns = pl.ds(tile * 256, 256)
        both = []
        for m in range(2):
            value = jnp.dot(gathered[0], gu[m, :HALF, columns], preferred_element_type=F32)
            both.append(value + jnp.dot(gathered[1], gu[m, HALF:, columns], preferred_element_type=F32))
        inner[:, columns] = (both[0] / (1.0 + jnp.exp(-both[0])) * both[1]).astype(BF)

    def down_product(half, core, target):
        rows = pl.ds(pl.multiple_of(core * 128, 128), 128)
        value = jnp.dot(inner[rows, :], wd[:, half * HALF : (half + 1) * HALF], preferred_element_type=F32)
        target[half] = value.astype(target.dtype)

    total, drain_last = reduce_scatter_z(
        me, down_product, sib_out.at[1], sib_in.at[1], own, ring_out.at[1], ring_in.at[1],
        rs_ring_send.at[1], rs_ring_recv.at[1], rs_sib_send.at[1], rs_sib_recv.at[1],
    )
    hidden_out[...] = (resid_keep[...].astype(F32) + jnp.concatenate(total, axis=1)).astype(BF)
    drain()
    drain_last()


VMEM_SPEC = pl.BlockSpec(memory_space=pltpu.VMEM)
ANY_SPEC = pl.BlockSpec(memory_space=pl.ANY)
DMA = pltpu.SemaphoreType.DMA


def on_device(tokens, attn_gain, mlp_gain, project_in, project_out, gate_up, project_down, kv_cache, lengths, owners, cache_start):
    half_index = np.arange(HD // 2, dtype=np.float32) * np.float32(2.0) / np.float32(HD)
    freqs = jnp.asarray(np.tile(np.float32(ROPE_BASE) ** -half_index, 4).astype(np.float32)[None, :])
    ints = [values.reshape(32, 128) for values in (lengths, owners, cache_start)]
    shape = jax.ShapeDtypeStruct
    compact, begin_col, end_col, end_row, sel, scat = pl.pallas_call(
        first_kernel,
        out_shape=(
            shape((SLOTS, 384), BF), shape((SLOTS, 128), F32), shape((SLOTS, 128), F32), shape((8, SLOTS), F32),
            shape((SLOTS, REQ), BF), shape((REQ, SLOTS), BF),
        ),
        in_specs=[VMEM_SPEC] * 6 + [ANY_SPEC],
        out_specs=(VMEM_SPEC,) * 6,
        scratch_shapes=[
            pltpu.VMEM((2, REQ, HALF), BF), pltpu.VMEM((D, 384), BF), pltpu.VMEM((REQ, 384), BF),
            pltpu.VMEM((NDP * BLK, 384), BF), pltpu.VMEM((NDP * BLK, 384), BF),
            DMA((2, 7)), DMA((2, 7)), DMA((16,)), DMA((16,)), DMA((15,)), DMA((15,)), DMA((3,)),
        ],
        compiler_params=pltpu.CompilerParams(collective_id=0, has_side_effects=True, vmem_limit_bytes=40 << 20),
        name="gather_project_route",
    )(tokens, attn_gain.reshape(1, D), *ints, freqs, project_in)

    whole = lambda *dims: pl.BlockSpec(dims, lambda s: (0,) * len(dims))
    kv_updated, ret = pl.pallas_call(
        middle_kernel,
        grid=(ROWS // PBLK,),
        out_shape=(shape((2, ROWS, 128), BF), shape((SLOTS, 256), BF)),
        in_specs=[
            whole(SLOTS, 384), whole(SLOTS, 128), whole(SLOTS, 128), whole(8, SLOTS),
            pl.BlockSpec((2, PBLK, 128), lambda s: (0, s, 0)),
        ],
        out_specs=(pl.BlockSpec((2, PBLK, 128), lambda s: (0, s, 0)), whole(SLOTS, 256)),
        scratch_shapes=[
            pltpu.VMEM((2 * SLOTS, 128), BF), pltpu.VMEM((2 * SLOTS, 128), F32), pltpu.VMEM((2 * SLOTS, 128), F32),
            pltpu.VMEM((2 * SLOTS, 128), F32),
        ],
        compiler_params=pltpu.CompilerParams(vmem_limit_bytes=40 << 20),
        name="attend_update",
    )(compact, begin_col, end_col, end_row, kv_cache)

    hidden_states, lse = pl.pallas_call(
        last_kernel,
        out_shape=(shape((BLK, D), BF), shape((2, REQ), F32)),
        in_specs=[VMEM_SPEC] * 5 + [ANY_SPEC] * 3,
        out_specs=(VMEM_SPEC,) * 2,
        scratch_shapes=[
            pltpu.VMEM((SLOTS, 256), BF), pltpu.VMEM((NDP * BLK, 256), BF), pltpu.VMEM((NDP * BLK, 256), BF),
            pltpu.VMEM((REQ, 128), BF), pltpu.VMEM((128, D), BF), pltpu.VMEM((2, D, FFL), BF), pltpu.VMEM((FFL, D), BF),
            pltpu.VMEM((2, REQ, HALF), BF), pltpu.VMEM((REQ, FFL), BF), pltpu.VMEM((BLK, D), BF),
            pltpu.VMEM((2, 2, 128, HALF), BF), pltpu.VMEM((2, 2, 128, HALF), BF), pltpu.VMEM((2, 128, HALF), F32),
            pltpu.VMEM((2, 2, 7, BLK, HALF), BF), pltpu.VMEM((2, 2, 7, BLK, HALF), BF),
            DMA((15,)), DMA((15,)), DMA((2, 7)), DMA((2, 7)), DMA((16,)), DMA((16,)),
            DMA((2, 2, 7)), DMA((2, 2, 7)), DMA((2, 2)), DMA((2, 2)), DMA((3,)),
        ],
        compiler_params=pltpu.CompilerParams(collective_id=1, has_side_effects=True, vmem_limit_bytes=48 << 20),
        name="return_project_mlp",
    )(tokens, mlp_gain.reshape(1, D), ret, sel, scat, project_out, gate_up, project_down)
    return hidden_states, lse.T, kv_updated


def solution(mesh):
    placed = (
        P(("dp", "tensor"), None),
        P(),
        P(),
        P(None, None, "tensor"),
        P("tensor", None),
        P(None, None, "tensor"),
        P("tensor", None),
        P(None, "dp", "tensor"),
        P(),
        P(),
        P(),
    )
    return jax.shard_map(
        on_device,
        mesh=mesh,
        in_specs=placed,
        out_specs=(P(("dp", "tensor"), None), P("dp", "tensor"), P(None, "dp", "tensor")),
        check_vma=False,
    )
```

time: 348 us -> 109 us (0.31); the launches traced: 344 us -> 109 us
  waiting for transfers between devices: 150 us -> 0 us
  local copies, waits for them, and re-layouts: 115 us -> 8.57 us
  Pallas kernels: 0 us -> 99.3 us
  matrix products: 24.2 us -> 0 us
  starting transfers between devices: 21.6 us -> 0 us
  other arithmetic: 17.9 us -> 0 us
  between operations: 15 us -> 0.7 us
    pallas_call x0 -> x3, Pallas kernels: none -> 99.3 us  [the longest x1 55.7 us: on_device(): pl.pallas_call(last_kernel, out_shape=(shape((BLK, D), BF), shape((2, REQ...]
    scatter x2 -> x0, local copies, waits for them, and re-layouts: 90.3 us -> none  [the longest x1 45.2 us: on_device(): kv_updated = kv_cache.at[0, write_rows].set(write_keys, mode='drop')]
    all_gather x2 -> x0, waiting for transfers between devices: 72.7 us -> none  [the longest x1 39.9 us: on_device(): lax.all_gather(scaled_norm(resid, mlp_gain), 'tensor', axis=0, tiled=True)]
    reduce_scatter x2 -> x0, waiting for transfers between devices: 52.3 us -> none  [the longest x1 52.3 us: on_device(): lax.psum_scatter(jnp.dot(attention, project_out, preferred_element_type=j...]
    all_to_all x4 -> x0, waiting for transfers between devices: 24.6 us -> none  [the longest x1 6.97 us: on_device(): lax.all_to_all(outgoing, 'dp', split_axis=0, concat_axis=0, tiled=True)]
    dot_general x18 -> x0, matrix products: 21.8 us -> none  [the longest x7 9.6 us: advance(): jnp.einsum('qhp,phe->qhe', weights, value_block, precision=lax.Precision....]
    all_to_all x4 -> x0, starting transfers between devices: 21.2 us -> none  [the longest x1 7.44 us: on_device(): lax.all_to_all(far_sum.reshape(groups, capacity, heads_local), 'dp', spli...]
    slice x15 -> x0, local copies, waits for them, and re-layouts: 7.93 us -> none  [the longest x7 6.96 us: advance(): window[1].reshape(block_rows, heads_local, head_size).astype(jnp.float32)]
  transfers between devices with their start and end apart: 8 -> 0, of which waited for: 7 -> 0; matrix products, arithmetic and copies ran while one was open for 30% -> 0% of each run, Pallas kernels for 0% -> 0%
where the time goes in v1:
time: 109 us
  Pallas kernels  99.3 us (91%)
  local copies, waits for them, and re-layouts  8.57 us (8%)
    pallas_call x1, Pallas kernels, on_device(): pl.pallas_call(last_kernel, out_shape=(shape((BLK, D), BF), shape((2, REQ...  55.7 us
    pallas_call x1, Pallas kernels, on_device(): pl.pallas_call(first_kernel, out_shape=(shape((SLOTS, 384), BF), shape((S...  28.8 us
    pallas_call x1, Pallas kernels, on_device(): pl.pallas_call(middle_kernel, grid=(ROWS // PBLK,), out_shape=(shape((2,...  14.8 us
    unnamed x24, local copies, waits for them, and re-layouts  7.87 us

profile of v1, /device:TPU:32, one launch (start us, length us, event | category | flops | bytes accessed | tf_op | source)
XLA Modules:
  0.0 108.6 jit_solution(12743195519792611220)
XLA Ops:
  0.6 0.7 reshape.22.gain
  1.3 0.0 copy-start.10
  1.3 0.0 copy-start.2
  1.3 1.4 %copy-done.2 = bf16[3,2048,128]{2,1,0:T(8,128)(2,1)S(1)} copy-done((bf16[3,2048,128]{2,1,0:T(8,128)(2,1)S(1)}, bf16[3,2048,128]{2,1,0:T(8,128)(2,1)}, u32[]{:S(2)}) %copy-start.2) | copy-done | bytes 1572888
  2.7 0.0 copy-start.4
  2.8 0.8 copy-done.4
  3.6 0.0 copy-start.6
  3.6 0.7 copy-done.6
  4.3 0.0 copy-start.7
  4.3 0.7 copy-done.7
  5.0 0.0 copy-start.8
  5.0 0.7 copy-done.8
  5.7 0.0 copy-start.9
  5.7 0.7 copy-done.9
  6.4 0.0 copy-start
  6.4 28.8 %gather_project_route.1 = (bf16[384,384]{1,0:T(8,128)(2,1)S(1)}, f32[384,128]{1,0:T(8,128)S(1)}, f32[384,128]{1,0:T(8,128)S(1)}, f32[8,384]{1,0:T(8,128)S(1)}, b...) custom-call(bf16[16,2048]{1,0:T(8,128)(2,1)S(1)} %copy-done.4, bf16[1,2048]{1,0:T(2,128)(2,1)S(1)} %reshape.22.gain, ...), custom_call_target="tpu_custom_call" | custom-call | tf_op jit(solution)/shard_map/gather_project_route/pallas_call | solution.py:458
  35.2 0.0 copy-start.1
  35.2 1.6 %copy-done.1 = bf16[2,4096,128]{2,1,0:T(8,128)(2,1)S(1)} copy-done((bf16[2,4096,128]{2,1,0:T(8,128)(2,1)S(1)}, bf16[2,4096,128]{2,1,0:T(8,128)(2,1)}, u32[]{:S(2)}) %copy-start.1) | copy-done | bytes 2097176
  36.8 0.0 copy-start.3
  36.8 0.0 copy-start.5
  36.8 14.8 %attend_update.1 = (bf16[2,4096,128]{2,1,0:T(8,128)(2,1)}, bf16[384,256]{1,0:T(8,128)(2,1)S(1)}) custom-call(bf16[384,384]{1,0:T(8,128)(2,1)S(1)} %get-tuple-element.13.compact, f32[384,128]{1,0:T(8,128)S(1)} %get-tuple-element.14.start_ref, f32[384,128]{1,0:T(8,128)S(1)} %get-tuple-element.15.end_ref, f32[8,384]{1,0:T(8,128)S(1)} %get-tuple-element.16.end_row, ...), custom_call_target="tpu_custom_call" | custom-call | tf_op jit(solution)/shard_map/attend_update/pallas_call | solution.py:476
  51.6 0.0 copy-done.10
  51.6 0.0 copy-done
  51.6 0.0 copy-done.3
  51.6 0.0 copy-done.5
  51.6 55.7 %return_project_mlp.1 = (bf16[16,2048]{1,0:T(8,128)(2,1)S(1)}, f32[2,256]{1,0:T(2,128)S(1)}) custom-call(bf16[16,2048]{1,0:T(8,128)(2,1)S(1)} %copy-done.5, bf16[1,2048]{1,0:T(2,128)(2,1)S(1)} %reshape.21.gain, bf16[384,256]{1,0:T(8,128)(2,1)S(1)} %get-tuple-element.17.ret, bf16[384,256]{1,0:T(8,128)(2,1)S(1)} %get-tuple-element.18.sel, ...), custom_call_target="tpu_custom_call" | custom-call | tf_op jit(solution)/shard_map/return_project_mlp/pallas_call | solution.py:493
  107.4 0.6 copy.17
  108.0 0.6 copy.18
  (1 shorter events, 0.0 us)
Async XLA Ops:
  1.3 50.3 %copy-start.10 = (bf16[2048]{0:T(1024)(128)(2,1)S(1)}, bf16[2048]{0:T(1024)(128)(2,1)}, u32[]{:S(2)}) copy-start(bf16[2048]{0:T(1024)(128)(2,1)} %param.14) | copy-start | bytes 12292
  1.3 1.4 %copy-start.2 = (bf16[3,2048,128]{2,1,0:T(8,128)(2,1)S(1)}, bf16[3,2048,128]{2,1,0:T(8,128)(2,1)}, u32[]{:S(2)}) copy-start(bf16[3,2048,128]{2,1,0:T(8,128)(2,1)} %w_hbm.1) | copy-start | bytes 4718596
  2.7 0.8 copy-start.4
  3.6 0.7 copy-start.6
  4.3 0.7 copy-start.7
  5.0 0.7 copy-start.8
  5.7 0.7 copy-start.9
  6.4 45.2 %copy-start = (bf16[512,2048]{1,0:T(8,128)(2,1)S(1)}, bf16[512,2048]{1,0:T(8,128)(2,1)}, u32[]{:S(2)}) copy-start(bf16[512,2048]{1,0:T(8,128)(2,1)} %wd_hbm.1) | copy-start | bytes 6291460
  35.2 1.6 %copy-start.1 = (bf16[2,4096,128]{2,1,0:T(8,128)(2,1)S(1)}, bf16[2,4096,128]{2,1,0:T(8,128)(2,1)}, u32[]{:S(2)}) copy-start(bf16[2,4096,128]{2,1,0:T(8,128)(2,1)} %cache.1) | copy-start | bytes 6291460
  36.8 14.8 %copy-start.3 = (bf16[128,2048]{1,0:T(8,128)(2,1)S(1)}, bf16[128,2048]{1,0:T(8,128)(2,1)}, u32[]{:S(2)}) copy-start(bf16[128,2048]{1,0:T(8,128)(2,1)} %wo_hbm.1) | copy-start | bytes 1572868
  36.8 14.8 %copy-start.5 = (bf16[16,2048]{1,0:T(8,128)(2,1)S(1)}, bf16[16,2048]{1,0:T(8,128)(2,1)}, u32[]{:S(2)}) copy-start(bf16[16,2048]{1,0:T(8,128)(2,1)} %tokens.3) | copy-start | bytes 196612

commit v2 on v1

v2 whole, which is shorter than its diff:
```python
import functools

import jax
import jax.numpy as jnp
import numpy as np
from jax import lax
from jax.experimental import pallas as pl
from jax.experimental.pallas import tpu as pltpu
from jax.sharding import PartitionSpec as P

MESH = pl.DeviceIdType.MESH
BF = jnp.bfloat16
F32 = jnp.float32
I32 = jnp.int32

EPS = 1e-05
ROPE_BASE = 130000.0
LOW = -1e30
HD = 64
NDP = 16
NTP = 16
NZ = 8
D = 2048
HALF = 1024
BLK = 16
REQ = 256
HOME = 128
SLOTS = HOME + NDP * BLK
ROWS = 4096
FFL = 512
PBLK = 1024

AG_RIGHT = ((1, 0), (1, 1), (2, 0), (2, 1), (3, 0), (3, 1), (4, 0))
AG_LEFT = ((1, 1), (1, 0), (2, 1), (2, 0), (3, 1), (3, 0), (4, 1))
RS_RIGHT = ((4, 0), (3, 1), (3, 0), (2, 1), (2, 0), (1, 1), (1, 0))
RS_LEFT = ((4, 1), (3, 0), (3, 1), (2, 0), (2, 1), (1, 0), (1, 1))


class Place:
    def __init__(self):
        self.d = lax.axis_index("dp")
        self.t = lax.axis_index("tensor")
        self.z = self.t // 2
        self.c = self.t % 2
        self.sib = (self.d, self.t + 1 - 2 * self.c)
        self.zdev = (
            (self.d, ((self.z + 1) % NZ) * 2 + self.c),
            (self.d, ((self.z + NZ - 1) % NZ) * 2 + self.c),
        )

    def dp_peer(self, offset):
        return (self.d + offset) % NDP


def greet(me):
    barrier = pltpu.get_barrier_semaphore()
    targets = [me.zdev[0], me.zdev[1], me.sib]
    targets += [(me.dp_peer(i), me.t) for i in range(1, NDP)]
    for target in targets:
        pl.semaphore_signal(barrier, inc=1, device_id=target, device_id_type=MESH)
    return lambda: pl.semaphore_wait(barrier, len(targets))


def iota(shape, axis):
    return lax.broadcasted_iota(I32, shape, axis)


def scaled_norm(wide, gain):
    factor = lax.rsqrt(jnp.mean(wide * wide, axis=-1, keepdims=True) + EPS)
    return (wide * factor * gain).astype(BF)


def all_gather_z(me, buf, row_of, ring_send, ring_recv, sib_send, sib_recv):
    lists = (AG_RIGHT, AG_LEFT)
    signs = (1, -1)
    sib_copies = []
    started = []

    def block(origin, half):
        return buf.at[half, pl.ds(pl.multiple_of(row_of(origin, me.c), BLK), BLK), :]

    def message(way, index):
        k, half = lists[way][index]
        origin = (me.z + NZ - signs[way] * (k - 1)) % NZ
        ref = block(origin, half)
        return pltpu.make_async_remote_copy(
            src_ref=ref, dst_ref=ref, send_sem=ring_send.at[way, index], recv_sem=ring_recv.at[way, index],
            device_id=me.zdev[way], device_id_type=MESH,
        )

    def sibling(origin, half):
        index = len(sib_copies)
        ref = block(origin, half)
        copy = pltpu.make_async_remote_copy(
            src_ref=ref, dst_ref=ref, send_sem=sib_send.at[index], recv_sem=sib_recv.at[index],
            device_id=me.sib, device_id_type=MESH,
        )
        copy.start()
        sib_copies.append(copy)

    def start(way, index):
        copy = message(way, index)
        copy.start()
        started.append(copy)

    def begin():
        for index in range(2):
            for way in range(2):
                start(way, index)
        for half in range(2):
            sibling(me.z, half)

    def finish():
        for index in range(7):
            for way in range(2):
                k, half = lists[way][index]
                message(way, index).wait_recv()
                if (k + 1, half) in lists[way]:
                    start(way, lists[way].index((k + 1, half)))
                sibling((me.z + NZ - signs[way] * k) % NZ, half)
        for copy in sib_copies:
            copy.wait_recv()

    def drain():
        for copy in started:
            copy.wait_send()
        for copy in sib_copies:
            copy.wait_send()

    return begin, finish, drain


def reduce_scatter_z(me, product, sib_out, sib_in, own, ring_out, ring_in, ring_send, ring_recv, sib_send, sib_recv):
    lists = (RS_RIGHT, RS_LEFT)
    signs = (1, -1)
    started = []

    def message(way, index):
        return pltpu.make_async_remote_copy(
            src_ref=ring_out.at[way, index], dst_ref=ring_in.at[way, index],
            send_sem=ring_send.at[way, index], recv_sem=ring_recv.at[way, index],
            device_id=me.zdev[way], device_id_type=MESH,
        )

    def mine(way, distance, half):
        target = (me.z + NZ + signs[way] * distance) % NZ
        return own[half, pl.ds(pl.multiple_of(target * BLK, BLK), BLK), :]

    def send(way, index, value):
        ring_out[way, index] = value.astype(BF)
        copy = message(way, index)
        copy.start()
        started.append(copy)

    for half in range(2):
        product(half, 1 - me.c, sib_out)
        copy = pltpu.make_async_remote_copy(
            src_ref=sib_out.at[half], dst_ref=sib_in.at[half], send_sem=sib_send.at[half], recv_sem=sib_recv.at[half],
            device_id=me.sib, device_id_type=MESH,
        )
        copy.start()
        started.append(copy)
        product(half, me.c, own)
    for half in range(2):
        started[half].wait_recv()
        own[half] = own[half] + sib_in[half].astype(F32)
        first = half
        send(first, 0, mine(first, 4, half))
        send(1 - first, 1, mine(1 - first, 3, half))
    total = [own[half, pl.ds(pl.multiple_of(me.z * BLK, BLK), BLK), :] for half in range(2)]
    for index in range(7):
        for way in range(2):
            distance, half = lists[way][index]
            message(way, index).wait_recv()
            arrived = ring_in[way, index].astype(F32)
            if distance > 1:
                send(way, lists[way].index((distance - 1, half)), arrived + mine(way, distance - 1, half))
            else:
                total[half] = total[half] + arrived
    return total, lambda: [copy.wait_send() for copy in started]


def exchange_dp(me, source, landing, send, recv):
    copies = []
    for i in range(1, NDP):
        peer = me.dp_peer(i)
        copy = pltpu.make_async_remote_copy(
            src_ref=source.at[pl.ds(pl.multiple_of(peer * BLK, BLK), BLK), :],
            dst_ref=landing.at[pl.ds(pl.multiple_of(me.d * BLK, BLK), BLK), :],
            send_sem=send.at[i - 1], recv_sem=recv.at[i - 1],
            device_id=(peer, me.t), device_id_type=MESH,
        )
        copy.start()
        copies.append(copy)
    here = pl.ds(pl.multiple_of(me.d * BLK, BLK), BLK)
    landing[here, :] = source[here, :]
    return copies


def column_of(row, hits):
    return jnp.sum(jnp.where(hits, row, 0.0), axis=1, keepdims=True)


def layer_kernel(
    tokens_hbm, attn_gain_hbm, mlp_gain_hbm, lengths_hbm, owners_hbm, starts_hbm, w_hbm, wo_hbm, gu_hbm, wd_hbm, cache_hbm,
    hidden_out, lse_out, cache_out,
    tokens, attn_gain, mlp_gain, ints, w, wo, gu, wd, cache,
    gathered, packed, compact, outgoing, sel, scat, begin_ref, end_ref, end_row,
    q2, top_ref, out_ref, ret_home, ret_away, landing, slots, attended, inner, resid_keep,
    sib_out, sib_in, own, ring_out, ring_in,
    dp_send, dp_recv, ag_ring_send, ag_ring_recv, ag_sib_send, ag_sib_recv,
    rs_ring_send, rs_ring_recv, rs_sib_send, rs_sib_recv, load_sem, store_sem,
):
    me = Place()
    pairs = [
        (tokens_hbm, tokens), (attn_gain_hbm, attn_gain), (owners_hbm, ints.at[0]), (lengths_hbm, ints.at[1]),
        (starts_hbm, ints.at[2]), (w_hbm.at[0], w.at[:, pl.ds(0, 128)]), (w_hbm.at[1], w.at[:, pl.ds(128, 128)]),
        (w_hbm.at[2], w.at[:, pl.ds(256, 128)]), (cache_hbm, cache), (wo_hbm, wo), (mlp_gain_hbm, mlp_gain), (gu_hbm, gu), (wd_hbm, wd),
    ]
    loads = [pltpu.make_async_copy(src, dst, load_sem.at[i]) for i, (src, dst) in enumerate(pairs)]
    for copy in loads:
        copy.start()
    wait_all = greet(me)
    loads[0].wait()
    loads[1].wait()

    def gain_row(ref):
        return jnp.concatenate([ref[i : i + 1, :].astype(F32) for i in range(16)], axis=1)

    normed = scaled_norm(tokens[...].astype(F32), gain_row(attn_gain))
    row_of = lambda zz, cc: (zz * 2 + cc) * BLK
    my_rows = pl.ds(pl.multiple_of(row_of(me.z, me.c), BLK), BLK)
    for half in range(2):
        gathered[0, half, my_rows, :] = normed[:, half * HALF : (half + 1) * HALF]
    wait_all()
    begin, finish, drain_gather = all_gather_z(
        me, gathered.at[0], row_of, ag_ring_send.at[0], ag_ring_recv.at[0], ag_sib_send.at[0], ag_sib_recv.at[0]
    )
    begin()

    for copy in loads[2:5]:
        copy.wait()

    def wide(m):
        return jnp.concatenate([ints[m, pl.ds(0, NDP, stride=2), :], ints[m, pl.ds(1, NDP, stride=2), :]], axis=1)

    def mine(m):
        return jnp.concatenate([ints[m, pl.ds(2 * me.d, 1), :], ints[m, pl.ds(2 * me.d + 1, 1), :]], axis=1)

    own_all, len_all, start_all = wide(0), wide(1), wide(2)
    own_row, len_row, start_row = mine(0), mine(1).astype(F32), mine(2).astype(F32)
    before = jnp.where(iota((REQ, REQ), 0) < iota((REQ, REQ), 1), 1.0, 0.0).astype(BF)
    here = own_all == me.d
    here_rank = jnp.dot(jnp.where(here, 1.0, 0.0).astype(BF), before, preferred_element_type=F32)
    away = here & (iota((NDP, REQ), 0) != me.d)
    place_in = jnp.where(away, here_rank, -1.0)
    onehot = jnp.where(iota((NDP, REQ), 0) == own_row, 1.0, 0.0)
    counts = jnp.dot(onehot.astype(BF), before, preferred_element_type=F32)
    rank = jnp.sum(onehot * counts, axis=0, keepdims=True)
    own_wide = own_row.astype(F32)
    place = jnp.where(own_row == me.d, rank, HOME + own_wide * BLK + rank)
    chosen = iota((SLOTS, REQ), 0).astype(F32) == place
    sel[...] = jnp.where(chosen, 1.0, 0.0).astype(BF)
    request = iota((REQ, REQ), 0)
    natural = ((request >> 4) & 7) * 32 + (request >> 7) * 16 + (request & 15)
    place_col = column_of(place, natural == iota((REQ, REQ), 1))
    scat[...] = jnp.where(iota((REQ, SLOTS), 1).astype(F32) == place_col, 1.0, 0.0).astype(BF)

    def spread(rows16):
        return jnp.concatenate(
            [jnp.broadcast_to(rows16[b : b + 1, :], (BLK, REQ)) for b in range(NDP)], axis=0
        )

    slot = (iota((NDP * BLK, REQ), 0) & (BLK - 1)).astype(F32)
    hits_in = spread(place_in) == slot
    begin_all = start_all.astype(F32)
    finish_all = begin_all + len_all.astype(F32)
    hits_home = chosen[:HOME]
    begin_col = jnp.concatenate(
        [column_of(start_row + 1.0, hits_home), column_of(spread(begin_all) + 1.0, hits_in)], axis=0
    ) - 1.0
    finish_col = jnp.concatenate(
        [column_of(start_row + len_row + 1.0, hits_home), column_of(spread(finish_all) + 1.0, hits_in)], axis=0
    ) - 1.0
    begin_ref[...] = jnp.broadcast_to(begin_col, (SLOTS, 128))
    end_ref[...] = jnp.broadcast_to(finish_col, (SLOTS, 128))
    eye = iota((SLOTS, SLOTS), 0) == iota((SLOTS, SLOTS), 1)
    end_row[...] = jnp.broadcast_to(jnp.sum(jnp.where(eye, finish_col, 0.0), axis=0, keepdims=True), (8, SLOTS))

    len_col = column_of(len_row, iota((REQ, REQ), 0) == iota((REQ, REQ), 1))
    lane = iota((1, 128), 1) & (HD // 2 - 1)
    freqs = jnp.exp(lane.astype(F32) * np.float32(-np.log(ROPE_BASE) / (HD // 2)))
    angle = len_col * freqs
    turns = jnp.floor(angle * (1.0 / (2.0 * np.pi)) + 0.5)
    left = (angle - turns * 6.28125) - turns * np.float32(2.0 * np.pi - 6.28125)
    x = 0.5 * left
    x2 = x * x
    sin_half = x * (1.0 + x2 * (-1 / 6 + x2 * (1 / 120 + x2 * (-1 / 5040 + x2 * (1 / 362880 - x2 / 39916800)))))
    cos_half = 1.0 + x2 * (
        -1 / 2 + x2 * (1 / 24 + x2 * (-1 / 720 + x2 * (1 / 40320 + x2 * (-1 / 3628800 + x2 / 479001600))))
    )
    sine = 2.0 * sin_half * cos_half
    cosine = 1.0 - 2.0 * sin_half * sin_half
    low_half = (iota((REQ, 128), 1) & (HD - 1)) < HD // 2
    signed = jnp.where(low_half, -sine, sine)

    finish()
    for copy in loads[5:8]:
        copy.wait()
    projected = jnp.dot(gathered[0, 0], w[:HALF], preferred_element_type=F32)
    projected = projected + jnp.dot(gathered[0, 1], w[HALF:], preferred_element_type=F32)

    def turned(values):
        partner = jnp.where(low_half, pltpu.roll(values, 96, 1), pltpu.roll(values, 32, 1))
        return (values * cosine + partner * signed).astype(BF)

    packed[:, 0:128] = turned(projected[:, 0:128])
    packed[:, 128:256] = turned(projected[:, 128:256])
    packed[:, 256:384] = projected[:, 256:384].astype(BF)
    outgoing[...] = jnp.dot(sel[HOME:, :], packed[...], preferred_element_type=F32).astype(BF)
    sent = exchange_dp(me, outgoing, compact.at[pl.ds(HOME, NDP * BLK), :], dp_send.at[0], dp_recv.at[0])
    compact[:HOME, :] = jnp.dot(sel[:HOME, :], packed[...], preferred_element_type=F32).astype(BF)
    loads[8].wait()

    def attend(first, count, ret):
        low_lanes = iota((count, 128), 1) < HD
        rows = pl.ds(first, count)
        q = compact[rows, 0:128].astype(F32) * (1.0 / 8.0)
        k = compact[rows, 128:256].astype(F32)
        v = compact[rows, 256:384].astype(F32)
        for head in range(2):
            keep = low_lanes if head == 0 else jnp.logical_not(low_lanes)
            qh = jnp.where(keep, q, 0.0)
            own_rows = pl.ds(head * count, count)
            q2[own_rows, :] = qh.astype(BF)
            top_ref[own_rows, :] = jnp.broadcast_to(jnp.sum(qh * k, axis=1, keepdims=True), (count, 128))
            out_ref[own_rows, 0:128] = v
            out_ref[own_rows, 128:256] = jnp.ones((count, 128), F32)

        @pl.loop(0, ROWS // PBLK)
        def _(block):
            base = pl.multiple_of(block * PBLK, PBLK)
            keys = cache[0, pl.ds(base, PBLK), :]
            values = jnp.concatenate([cache[1, pl.ds(base, PBLK), :], jnp.ones((PBLK, 128), BF)], axis=1)
            across = (iota((1, PBLK), 1) + base).astype(F32)
            live = (across >= begin_ref[rows, 0:1]) & (across < end_ref[rows, 0:1])
            for head in range(2):
                own_rows = pl.ds(head * count, count)
                scores = lax.dot_general(q2[own_rows, :], keys, (((1,), (1,)), ((), ())), preferred_element_type=F32)
                scores = jnp.where(live, scores, LOW)
                old_top = top_ref[own_rows, 0:1]
                top = jnp.maximum(old_top, jnp.max(scores, axis=1, keepdims=True))
                weights = jnp.exp(scores - top).astype(BF)
                added = jnp.dot(weights, values, preferred_element_type=F32)
                out_ref[own_rows, :] = out_ref[own_rows, :] * jnp.exp(old_top - top) + added
                top_ref[own_rows, :] = jnp.broadcast_to(top, (count, 128))

        first_rows, second_rows = pl.ds(0, count), pl.ds(count, count)
        upper = jnp.where(low_lanes, out_ref[first_rows, 0:128], out_ref[second_rows, 0:128])
        lower = jnp.where(low_lanes, out_ref[first_rows, 128:256], out_ref[second_rows, 128:256])
        ret[:, 0:128] = (upper / lower).astype(BF)
        lse = [top_ref[r, :] + jnp.log(out_ref[r, 128:256]) for r in (first_rows, second_rows)]
        high = [value.astype(BF).astype(F32) for value in lse]
        low = [a - b for a, b in zip(lse, high)]
        lane = iota((count, 128), 1)
        tail = jnp.where(lane == 0, high[0], jnp.where(lane == 1, low[0], jnp.where(lane == 2, high[1], low[1])))
        ret[:, 128:256] = tail.astype(BF)

    attend(0, HOME, ret_home)
    drain_gather()
    for copy in sent:
        copy.wait_recv()
    attend(HOME, NDP * BLK, ret_away)
    back = exchange_dp(me, ret_away, landing, dp_send.at[1], dp_recv.at[1])

    @pl.loop(0, ROWS // PBLK)
    def _(block):
        base = pl.multiple_of(block * PBLK, PBLK)
        span = pl.ds(base, PBLK)
        position = (iota((PBLK, SLOTS), 0) + base).astype(F32)
        written = jnp.where(position == end_row[0:1, :], 1.0, 0.0)
        hit = jnp.max(written, axis=1, keepdims=True) > 0.5
        fresh = jnp.dot(written.astype(BF), compact[:, 128:384], preferred_element_type=F32)
        cache[0, span, :] = jnp.where(hit, fresh[:, 0:128], cache[0, span, :].astype(F32)).astype(BF)
        cache[1, span, :] = jnp.where(hit, fresh[:, 128:256], cache[1, span, :].astype(F32)).astype(BF)

    store = pltpu.make_async_copy(cache, cache_out, store_sem.at[0])
    store.start()
    slots[:HOME, :] = ret_home[...]
    loads[9].wait()
    for copy in back:
        copy.wait_recv()
    slots[HOME:, :] = landing[...]
    attended[...] = jnp.dot(scat[...], slots[:, 0:128], preferred_element_type=F32).astype(BF)

    def out_product(half, core, target):
        rows = pl.ds(pl.multiple_of(core * 128, 128), 128)
        value = jnp.dot(attended[rows, :], wo[:, half * HALF : (half + 1) * HALF], preferred_element_type=F32)
        target[half] = value.astype(target.dtype)

    total, drain_first = reduce_scatter_z(
        me, out_product, sib_out.at[0], sib_in.at[0], own, ring_out.at[0], ring_in.at[0],
        rs_ring_send.at[0], rs_ring_recv.at[0], rs_sib_send.at[0], rs_sib_recv.at[0],
    )
    resid = (tokens[...].astype(F32) + jnp.concatenate(total, axis=1)).astype(BF)
    resid_keep[...] = resid
    loads[10].wait()
    normed = scaled_norm(resid.astype(F32), gain_row(mlp_gain))
    row_of_core = lambda zz, cc: cc * 128 + zz * BLK
    my_rows = pl.ds(pl.multiple_of(row_of_core(me.z, me.c), BLK), BLK)
    for half in range(2):
        gathered[1, half, my_rows, :] = normed[:, half * HALF : (half + 1) * HALF]
    begin, finish_mlp, drain_mlp = all_gather_z(
        me, gathered.at[1], row_of_core, ag_ring_send.at[1], ag_ring_recv.at[1], ag_sib_send.at[1], ag_sib_recv.at[1]
    )
    begin()
    spread_sel = sel[...].astype(F32)
    tail = slots[:, 128:256].astype(F32)
    for head in range(2):
        lse = tail[:, 2 * head : 2 * head + 1] + tail[:, 2 * head + 1 : 2 * head + 2]
        lse_out[head : head + 1, :] = jnp.sum(spread_sel * lse, axis=0, keepdims=True)
    drain_first()
    for copy in sent + back:
        copy.wait_send()
    loads[11].wait()
    loads[12].wait()
    finish_mlp()
    for tile in range(FFL // 256):
        columns = pl.ds(tile * 256, 256)
        both = []
        for m in range(2):
            value = jnp.dot(gathered[1, 0], gu[m, :HALF, columns], preferred_element_type=F32)
            both.append(value + jnp.dot(gathered[1, 1], gu[m, HALF:, columns], preferred_element_type=F32))
        inner[:, columns] = (both[0] / (1.0 + jnp.exp(-both[0])) * both[1]).astype(BF)

    def down_product(half, core, target):
        rows = pl.ds(pl.multiple_of(core * 128, 128), 128)
        value = jnp.dot(inner[rows, :], wd[:, half * HALF : (half + 1) * HALF], preferred_element_type=F32)
        target[half] = value.astype(target.dtype)

    total, drain_last = reduce_scatter_z(
        me, down_product, sib_out.at[1], sib_in.at[1], own, ring_out.at[1], ring_in.at[1],
        rs_ring_send.at[1], rs_ring_recv.at[1], rs_sib_send.at[1], rs_sib_recv.at[1],
    )
    hidden_out[...] = (resid_keep[...].astype(F32) + jnp.concatenate(total, axis=1)).astype(BF)
    drain_mlp()
    drain_last()
    store.wait()


VMEM_SPEC = pl.BlockSpec(memory_space=pltpu.VMEM)
ANY_SPEC = pl.BlockSpec(memory_space=pl.ANY)
DMA = pltpu.SemaphoreType.DMA


def on_device(tokens, attn_gain, mlp_gain, project_in, project_out, gate_up, project_down, kv_cache, lengths, owners, cache_start):
    shape = jax.ShapeDtypeStruct
    hidden_states, lse, kv_updated = pl.pallas_call(
        layer_kernel,
        out_shape=(shape((BLK, D), BF), shape((2, REQ), F32), shape((2, ROWS, 128), BF)),
        in_specs=[ANY_SPEC] * 11,
        out_specs=(VMEM_SPEC, VMEM_SPEC, ANY_SPEC),
        scratch_shapes=[
            pltpu.VMEM((BLK, D), BF), pltpu.VMEM((16, 128), BF), pltpu.VMEM((16, 128), BF), pltpu.VMEM((3, 32, 128), I32),
            pltpu.VMEM((D, 384), BF), pltpu.VMEM((128, D), BF), pltpu.VMEM((2, D, FFL), BF), pltpu.VMEM((FFL, D), BF),
            pltpu.VMEM((2, ROWS, 128), BF),
            pltpu.VMEM((2, 2, REQ, HALF), BF), pltpu.VMEM((REQ, 384), BF), pltpu.VMEM((SLOTS, 384), BF),
            pltpu.VMEM((NDP * BLK, 384), BF), pltpu.VMEM((SLOTS, REQ), BF), pltpu.VMEM((REQ, SLOTS), BF),
            pltpu.VMEM((SLOTS, 128), F32), pltpu.VMEM((SLOTS, 128), F32), pltpu.VMEM((8, SLOTS), F32),
            pltpu.VMEM((512, 128), BF), pltpu.VMEM((512, 128), F32), pltpu.VMEM((512, 256), F32),
            pltpu.VMEM((HOME, 256), BF), pltpu.VMEM((NDP * BLK, 256), BF), pltpu.VMEM((NDP * BLK, 256), BF),
            pltpu.VMEM((SLOTS, 256), BF), pltpu.VMEM((REQ, 128), BF), pltpu.VMEM((REQ, FFL), BF), pltpu.VMEM((BLK, D), BF),
            pltpu.VMEM((2, 2, 128, HALF), BF), pltpu.VMEM((2, 2, 128, HALF), BF), pltpu.VMEM((2, 128, HALF), F32),
            pltpu.VMEM((2, 2, 7, BLK, HALF), BF), pltpu.VMEM((2, 2, 7, BLK, HALF), BF),
            DMA((2, 15)), DMA((2, 15)), DMA((2, 2, 7)), DMA((2, 2, 7)), DMA((2, 16)), DMA((2, 16)),
            DMA((2, 2, 7)), DMA((2, 2, 7)), DMA((2, 2)), DMA((2, 2)), DMA((13,)), DMA((1,)),
        ],
        compiler_params=pltpu.CompilerParams(collective_id=0, has_side_effects=True, vmem_limit_bytes=56 << 20),
        name="decode_layer",
    )(
        tokens, attn_gain.reshape(16, 128), mlp_gain.reshape(16, 128), lengths.reshape(32, 128), owners.reshape(32, 128),
        cache_start.reshape(32, 128), project_in, project_out, gate_up, project_down, kv_cache,
    )
    return hidden_states, lse.T, kv_updated


def solution(mesh):
    placed = (
        P(("dp", "tensor"), None),
        P(),
        P(),
        P(None, None, "tensor"),
        P("tensor", None),
        P(None, None, "tensor"),
        P("tensor", None),
        P(None, "dp", "tensor"),
        P(),
        P(),
        P(),
    )
    return jax.shard_map(
        on_device,
        mesh=mesh,
        in_specs=placed,
        out_specs=(P(("dp", "tensor"), None), P("dp", "tensor"), P(None, "dp", "tensor")),
        check_vma=False,
    )
```

time: 109 us -> 95 us (0.87)
  Pallas kernels: 99.3 us -> 88.5 us
  local copies, waits for them, and re-layouts: 8.57 us -> 5.76 us
    pallas_call x3 -> x1, Pallas kernels: 99.3 us -> 88.5 us  [on_device(): pl.pallas_call(layer_kernel, out_shape=(shape((BLK, D), BF), shape((2, RE...]
    unnamed x24 -> x3, local copies, waits for them, and re-layouts: 7.87 us -> 5.76 us
where the time goes in v2:
time: 95 us; the launch traced here: 94.9 us
  Pallas kernels  88.5 us (93%)
  local copies, waits for them, and re-layouts  5.76 us (6%)
    pallas_call x1, Pallas kernels, on_device(): pl.pallas_call(layer_kernel, out_shape=(shape((BLK, D), BF), shape((2, RE...  88.5 us
    unnamed x3, local copies, waits for them, and re-layouts  5.76 us

profile of v2, /device:TPU:32, one launch (start us, length us, event | category | flops | bytes accessed | tf_op | source)
XLA Modules:
  0.0 94.9 jit_solution(10566051671240397713)
XLA Ops:
  0.6 88.5 %decode_layer.1 = (bf16[16,2048]{1,0:T(8,128)(2,1)}, f32[2,256]{1,0:T(2,128)}, bf16[2,4096,128]{2,1,0:T(8,128)(2,1)}) custom-call(bf16[16,2048]{1,0:T(8,128)(2,1)} %tokens_hbm.1, bf16[16,128]{1,0:T(8,128)(2,1)} %bitcast.9, bf16[16,128]{1,0:T(8,128)(2,1)} %bitcast.10, s32[32,128]{1,0:T(8,128)} %bitcast.6, s32[32,128]{1,0:T(8,128)} %bitcast.7, ...), custom_call_target="tpu_custom_call" | custom-call | tf_op jit(solution)/shard_map/decode_layer/pallas_call | solution.py:458
  89.1 1.5 %copy.17 = bf16[16,2048]{1,0:T(8,128)(2,1)} copy(bf16[16,2048]{1,0:T(8,128)(2,1)} %get-tuple-element.12) | data formatting | bytes 131072
  90.6 1.2 %copy.18 = f32[256,2]{0,1:T(2,128)} copy(f32[256,2]{0,1:T(2,128)} %bitcast.11) | data formatting | bytes 4096
  91.8 3.0 %copy.19 = bf16[2,4096,128]{2,1,0:T(8,128)(2,1)} copy(bf16[2,4096,128]{2,1,0:T(8,128)(2,1)} %get-tuple-element.14) | data formatting | bytes 4194304

commit v3 on v2

--- a/solution.py
+++ b/solution.py
@@ -30,11 +30,6 @@
 FFL = 512
 PBLK = 1024
 
-AG_RIGHT = ((1, 0), (1, 1), (2, 0), (2, 1), (3, 0), (3, 1), (4, 0))
-AG_LEFT = ((1, 1), (1, 0), (2, 1), (2, 0), (3, 1), (3, 0), (4, 1))
-RS_RIGHT = ((4, 0), (3, 1), (3, 0), (2, 1), (2, 0), (1, 1), (1, 0))
-RS_LEFT = ((4, 1), (3, 0), (3, 1), (2, 0), (2, 1), (1, 0), (1, 1))
-
 
 class Place:
     def __init__(self):
@@ -43,10 +38,9 @@
         self.z = self.t // 2
         self.c = self.t % 2
         self.sib = (self.d, self.t + 1 - 2 * self.c)
-        self.zdev = (
-            (self.d, ((self.z + 1) % NZ) * 2 + self.c),
-            (self.d, ((self.z + NZ - 1) % NZ) * 2 + self.c),
-        )
+
+    def along_z(self, offset):
+        return (self.d, ((self.z + NZ + offset) % NZ) * 2 + self.c)
 
     def dp_peer(self, offset):
         return (self.d + offset) % NDP
@@ -54,7 +48,7 @@
 
 def greet(me):
     barrier = pltpu.get_barrier_semaphore()
-    targets = [me.zdev[0], me.zdev[1], me.sib]
+    targets = [me.along_z(k) for k in (1, -1, 2, -2)] + [me.sib]
     targets += [(me.dp_peer(i), me.t) for i in range(1, NDP)]
     for target in targets:
         pl.semaphore_signal(barrier, inc=1, device_id=target, device_id_type=MESH)
@@ -70,25 +64,31 @@
     return (wide * factor * gain).astype(BF)
 
 
-def all_gather_z(me, buf, row_of, ring_send, ring_recv, sib_send, sib_recv):
-    lists = (AG_RIGHT, AG_LEFT)
+def gather_z(me, buf, row_of, send, recv, sib_send=None, sib_recv=None):
     signs = (1, -1)
+    started = []
     sib_copies = []
-    started = []
+    kinds = lambda way: ((2, 0, 2), (2, 1, 2), (1, 0, 1), (1, 1, 1), (3, 0, 1), (3, 1, 1), (4, way, 2))
 
     def block(origin, half):
         return buf.at[half, pl.ds(pl.multiple_of(row_of(origin, me.c), BLK), BLK), :]
 
     def message(way, index):
-        k, half = lists[way][index]
-        origin = (me.z + NZ - signs[way] * (k - 1)) % NZ
-        ref = block(origin, half)
+        distance, half, hops = kinds(way)[index]
+        ref = block((me.z + NZ - signs[way] * (distance - hops)) % NZ, half)
         return pltpu.make_async_remote_copy(
-            src_ref=ref, dst_ref=ref, send_sem=ring_send.at[way, index], recv_sem=ring_recv.at[way, index],
-            device_id=me.zdev[way], device_id_type=MESH,
+            src_ref=ref, dst_ref=ref, send_sem=send.at[way, index], recv_sem=recv.at[way, index],
+            device_id=me.along_z(signs[way] * hops), device_id_type=MESH,
         )
 
+    def start(way, index):
+        copy = message(way, index)
+        copy.start()
+        started.append(copy)
+
     def sibling(origin, half):
+        if sib_send is None:
+            return
         index = len(sib_copies)
         ref = block(origin, half)
         copy = pltpu.make_async_remote_copy(
@@ -98,85 +98,81 @@
         copy.start()
         sib_copies.append(copy)
 
-    def start(way, index):
-        copy = message(way, index)
-        copy.start()
-        started.append(copy)
-
     def begin():
-        for index in range(2):
+        for index in range(4):
             for way in range(2):
-                start(way, index)
+                start(way, index ^ way if index < 2 else index)
         for half in range(2):
             sibling(me.z, half)
 
+    def arrive(way, index):
+        message(way, index).wait_recv()
+        distance, half, _ = kinds(way)[index]
+        if distance == 2:
+            if half == way:
+                start(way, 6)
+            start(way, 4 + half)
+        sibling((me.z + NZ - signs[way] * distance) % NZ, half)
+
     def finish():
-        for index in range(7):
+        for index in (0, 1, 2, 3, 4, 5, 6):
             for way in range(2):
-                k, half = lists[way][index]
-                message(way, index).wait_recv()
-                if (k + 1, half) in lists[way]:
-                    start(way, lists[way].index((k + 1, half)))
-                sibling((me.z + NZ - signs[way] * k) % NZ, half)
+                arrive(way, index if index in (2, 3, 6) else index ^ way)
         for copy in sib_copies:
             copy.wait_recv()
 
     def drain():
-        for copy in started:
+        for copy in started + sib_copies:
             copy.wait_send()
-        for copy in sib_copies:
-            copy.wait_send()
 
     return begin, finish, drain
 
 
-def reduce_scatter_z(me, product, sib_out, sib_in, own, ring_out, ring_in, ring_send, ring_recv, sib_send, sib_recv):
-    lists = (RS_RIGHT, RS_LEFT)
+def reduce_z(me, product, own, out, landed, send, recv):
     signs = (1, -1)
+    hops = (1, 1, 2, 2, 2, 1, 1)
     started = []
 
     def message(way, index):
         return pltpu.make_async_remote_copy(
-            src_ref=ring_out.at[way, index], dst_ref=ring_in.at[way, index],
-            send_sem=ring_send.at[way, index], recv_sem=ring_recv.at[way, index],
-            device_id=me.zdev[way], device_id_type=MESH,
+            src_ref=out.at[way, index], dst_ref=landed.at[way, index],
+            send_sem=send.at[way, index], recv_sem=recv.at[way, index],
+            device_id=me.along_z(signs[way] * hops[index]), device_id_type=MESH,
         )
 
-    def mine(way, distance, half):
-        target = (me.z + NZ + signs[way] * distance) % NZ
+    def mine(offset, half):
+        target = (me.z + NZ + offset) % NZ
         return own[half, pl.ds(pl.multiple_of(target * BLK, BLK), BLK), :]
 
-    def send(way, index, value):
-        ring_out[way, index] = value.astype(BF)
+    def go(way, index, value):
+        out[way, index] = value.astype(BF)
         copy = message(way, index)
         copy.start()
         started.append(copy)
 
+    def landed_sum(way, index):
+        message(way, index).wait_recv()
+        return landed[way, index].astype(F32)
+
     for half in range(2):
-        product(half, 1 - me.c, sib_out)
-        copy = pltpu.make_async_remote_copy(
-            src_ref=sib_out.at[half], dst_ref=sib_in.at[half], send_sem=sib_send.at[half], recv_sem=sib_recv.at[half],
-            device_id=me.sib, device_id_type=MESH,
-        )
-        copy.start()
-        started.append(copy)
-        product(half, me.c, own)
+        own[half] = product(half)
+        go(half, 2, mine(4 * signs[half], half))
+        for way in range(2):
+            go(way, half, mine(3 * signs[way], half))
     for half in range(2):
-        started[half].wait_recv()
-        own[half] = own[half] + sib_in[half].astype(F32)
-        first = half
-        send(first, 0, mine(first, 4, half))
-        send(1 - first, 1, mine(1 - first, 3, half))
-    total = [own[half, pl.ds(pl.multiple_of(me.z * BLK, BLK), BLK), :] for half in range(2)]
-    for index in range(7):
         for way in range(2):
-            distance, half = lists[way][index]
-            message(way, index).wait_recv()
-            arrived = ring_in[way, index].astype(F32)
-            if distance > 1:
-                send(way, lists[way].index((distance - 1, half)), arrived + mine(way, distance - 1, half))
-            else:
-                total[half] = total[half] + arrived
+            go(way, 5 + half, mine(signs[way], half))
+    total = [mine(0, half) for half in range(2)]
+    for half in range(2):
+        for way in (1 - half, half):
+            value = landed_sum(way, half) + mine(2 * signs[way], half)
+            if half == way:
+                value = value + landed_sum(way, 2)
+            go(way, 3 + half, value)
+    for base in (5, 3):
+        for half in range(2):
+            for way in range(2):
+                total[half] = total[half] + landed_sum(way, base + half)
     return total, lambda: [copy.wait_send() for copy in started]
 
 
@@ -205,17 +201,16 @@
     tokens_hbm, attn_gain_hbm, mlp_gain_hbm, lengths_hbm, owners_hbm, starts_hbm, w_hbm, wo_hbm, gu_hbm, wd_hbm, cache_hbm,
     hidden_out, lse_out, cache_out,
     tokens, attn_gain, mlp_gain, ints, w, wo, gu, wd, cache,
-    gathered, packed, compact, outgoing, sel, scat, begin_ref, end_ref, end_row,
+    gathered, gathered_mlp, packed, compact, outgoing, sel, scat, begin_ref, end_ref, end_row,
     q2, top_ref, out_ref, ret_home, ret_away, landing, slots, attended, inner, resid_keep,
-    sib_out, sib_in, own, ring_out, ring_in,
-    dp_send, dp_recv, ag_ring_send, ag_ring_recv, ag_sib_send, ag_sib_recv,
-    rs_ring_send, rs_ring_recv, rs_sib_send, rs_sib_recv, load_sem, store_sem,
+    own, ring_out, ring_in,
+    dp_send, dp_recv, ag_send, ag_recv, ag_sib_send, ag_sib_recv, rs_send, rs_recv, core_send, core_recv, load_sem, store_sem,
 ):
     me = Place()
     pairs = [
         (tokens_hbm, tokens), (attn_gain_hbm, attn_gain), (owners_hbm, ints.at[0]), (lengths_hbm, ints.at[1]),
         (starts_hbm, ints.at[2]), (w_hbm.at[0], w.at[:, pl.ds(0, 128)]), (w_hbm.at[1], w.at[:, pl.ds(128, 128)]),
-        (w_hbm.at[2], w.at[:, pl.ds(256, 128)]), (cache_hbm, cache), (wo_hbm, wo), (mlp_gain_hbm, mlp_gain), (gu_hbm, gu), (wd_hbm, wd),
+        (w_hbm.at[2], w.at[:, pl.ds(256, 128)]), (cache_hbm, cache), (wo_hbm, wo.at[0]), (mlp_gain_hbm, mlp_gain), (gu_hbm, gu.at[0]), (wd_hbm, wd.at[0]),
     ]
     loads = [pltpu.make_async_copy(src, dst, load_sem.at[i]) for i, (src, dst) in enumerate(pairs)]
     for copy in loads:
@@ -231,10 +226,10 @@
     row_of = lambda zz, cc: (zz * 2 + cc) * BLK
     my_rows = pl.ds(pl.multiple_of(row_of(me.z, me.c), BLK), BLK)
     for half in range(2):
-        gathered[0, half, my_rows, :] = normed[:, half * HALF : (half + 1) * HALF]
+        gathered[half, my_rows, :] = normed[:, half * HALF : (half + 1) * HALF]
     wait_all()
-    begin, finish, drain_gather = all_gather_z(
-        me, gathered.at[0], row_of, ag_ring_send.at[0], ag_ring_recv.at[0], ag_sib_send.at[0], ag_sib_recv.at[0]
+    begin, finish, drain_gather = gather_z(
+        me, gathered, row_of, ag_send.at[0], ag_recv.at[0], ag_sib_send, ag_sib_recv
     )
     begin()
 
@@ -305,10 +300,19 @@
     signed = jnp.where(low_half, -sine, sine)
 
     finish()
+
+    def to_core(src, dst, index):
+        copy = pltpu.make_async_remote_copy(
+            src_ref=src, dst_ref=dst, send_sem=core_send.at[index], recv_sem=core_recv.at[index],
+            device_id=me.sib, device_id_type=MESH,
+        )
+        copy.start()
+        return copy
+
     for copy in loads[5:8]:
         copy.wait()
-    projected = jnp.dot(gathered[0, 0], w[:HALF], preferred_element_type=F32)
-    projected = projected + jnp.dot(gathered[0, 1], w[HALF:], preferred_element_type=F32)
+    projected = jnp.dot(gathered[0], w[:HALF], preferred_element_type=F32)
+    projected = projected + jnp.dot(gathered[1], w[HALF:], preferred_element_type=F32)
 
     def turned(values):
         partner = jnp.where(low_half, pltpu.roll(values, 96, 1), pltpu.roll(values, 32, 1))
@@ -320,6 +324,7 @@
     outgoing[...] = jnp.dot(sel[HOME:, :], packed[...], preferred_element_type=F32).astype(BF)
     sent = exchange_dp(me, outgoing, compact.at[pl.ds(HOME, NDP * BLK), :], dp_send.at[0], dp_recv.at[0])
     compact[:HOME, :] = jnp.dot(sel[:HOME, :], packed[...], preferred_element_type=F32).astype(BF)
+    shared = [to_core(wo_hbm, wo.at[1], 0), to_core(gu_hbm, gu.at[1], 1), to_core(wd_hbm, wd.at[1], 2)]
     loads[8].wait()
 
     def attend(first, count, ret):
@@ -391,28 +396,34 @@
     for copy in back:
         copy.wait_recv()
     slots[HOME:, :] = landing[...]
-    attended[...] = jnp.dot(scat[...], slots[:, 0:128], preferred_element_type=F32).astype(BF)
-
-    def out_product(half, core, target):
+
+    def assemble(core):
         rows = pl.ds(pl.multiple_of(core * 128, 128), 128)
-        value = jnp.dot(attended[rows, :], wo[:, half * HALF : (half + 1) * HALF], preferred_element_type=F32)
-        target[half] = value.astype(target.dtype)
-
-    total, drain_first = reduce_scatter_z(
-        me, out_product, sib_out.at[0], sib_in.at[0], own, ring_out.at[0], ring_in.at[0],
-        rs_ring_send.at[0], rs_ring_recv.at[0], rs_sib_send.at[0], rs_sib_recv.at[0],
+        return jnp.dot(scat[rows, :], slots[:, 0:128], preferred_element_type=F32).astype(BF)
+
+    attended[2] = assemble(1 - me.c)
+    swapped = to_core(attended.at[2], attended.at[1], 3)
+    attended[0] = assemble(me.c)
+    shared[0].wait_recv()
+    swapped.wait_recv()
+
+    def out_product(half):
+        columns = pl.ds(half * HALF, HALF)
+        value = jnp.dot(attended[0], wo[0, :, columns], preferred_element_type=F32)
+        return value + jnp.dot(attended[1], wo[1, :, columns], preferred_element_type=F32)
+
+    total, drain_first = reduce_z(
+        me, out_product, own.at[0], ring_out.at[0], ring_in.at[0], rs_send.at[0], rs_recv.at[0]
     )
     resid = (tokens[...].astype(F32) + jnp.concatenate(total, axis=1)).astype(BF)
     resid_keep[...] = resid
     loads[10].wait()
     normed = scaled_norm(resid.astype(F32), gain_row(mlp_gain))
-    row_of_core = lambda zz, cc: cc * 128 + zz * BLK
-    my_rows = pl.ds(pl.multiple_of(row_of_core(me.z, me.c), BLK), BLK)
+    row_of_chip = lambda zz, cc: zz * BLK
+    my_rows = pl.ds(pl.multiple_of(me.z * BLK, BLK), BLK)
     for half in range(2):
-        gathered[1, half, my_rows, :] = normed[:, half * HALF : (half + 1) * HALF]
-    begin, finish_mlp, drain_mlp = all_gather_z(
-        me, gathered.at[1], row_of_core, ag_ring_send.at[1], ag_ring_recv.at[1], ag_sib_send.at[1], ag_sib_recv.at[1]
-    )
+        gathered_mlp[half, my_rows, :] = normed[:, half * HALF : (half + 1) * HALF]
+    begin, finish_mlp, drain_mlp = gather_z(me, gathered_mlp, row_of_chip, ag_send.at[1], ag_recv.at[1])
     begin()
     spread_sel = sel[...].astype(F32)
     tail = slots[:, 128:256].astype(F32)
@@ -424,28 +435,45 @@
         copy.wait_send()
     loads[11].wait()
     loads[12].wait()
+    shared[1].wait_recv()
+    shared[2].wait_recv()
     finish_mlp()
-    for tile in range(FFL // 256):
-        columns = pl.ds(tile * 256, 256)
-        both = []
-        for m in range(2):
-            value = jnp.dot(gathered[1, 0], gu[m, :HALF, columns], preferred_element_type=F32)
-            both.append(value + jnp.dot(gathered[1, 1], gu[m, HALF:, columns], preferred_element_type=F32))
-        inner[:, columns] = (both[0] / (1.0 + jnp.exp(-both[0])) * both[1]).astype(BF)
-
-    def down_product(half, core, target):
-        rows = pl.ds(pl.multiple_of(core * 128, 128), 128)
-        value = jnp.dot(inner[rows, :], wd[:, half * HALF : (half + 1) * HALF], preferred_element_type=F32)
-        target[half] = value.astype(target.dtype)
-
-    total, drain_last = reduce_scatter_z(
-        me, down_product, sib_out.at[1], sib_in.at[1], own, ring_out.at[1], ring_in.at[1],
-        rs_ring_send.at[1], rs_ring_recv.at[1], rs_sib_send.at[1], rs_sib_recv.at[1],
+    for core in range(2):
+        for tile in range(FFL // 256):
+            columns = pl.ds(tile * 256, 256)
+            both = []
+            for m in range(2):
+                value = jnp.dot(gathered_mlp[0], gu[core, m, :HALF, columns], preferred_element_type=F32)
+                both.append(value + jnp.dot(gathered_mlp[1], gu[core, m, HALF:, columns], preferred_element_type=F32))
+            inner[core, :, columns] = (both[0] / (1.0 + jnp.exp(-both[0])) * both[1]).astype(BF)
+
+    def down_product(half):
+        columns = pl.ds(half * HALF, HALF)
+        value = jnp.dot(inner[0], wd[0, :, columns], preferred_element_type=F32)
+        return value + jnp.dot(inner[1], wd[1, :, columns], preferred_element_type=F32)
+
+    total, drain_last = reduce_z(
+        me, down_product, own.at[1], ring_out.at[1], ring_in.at[1], rs_send.at[1], rs_recv.at[1]
     )
     hidden_out[...] = (resid_keep[...].astype(F32) + jnp.concatenate(total, axis=1)).astype(BF)
     drain_mlp()
     drain_last()
+    for copy in shared:
+        copy.wait_send()
+    swapped.wait_send()
     store.wait()
+
+
+def store_kernel(hidden, lse, cache, hidden_out, lse_out, cache_out, sems):
+    pairs = [(hidden, hidden_out), (lse, lse_out)]
+    for part in range(8):
+        span = pl.ds(part % 4 * (ROWS // 4), ROWS // 4)
+        pairs.append((cache.at[part // 4, span], cache_out.at[part // 4, span]))
+    copies = [pltpu.make_async_copy(src, dst, sems.at[i]) for i, (src, dst) in enumerate(pairs)]
+    for copy in copies:
+        copy.start()
+    for copy in copies:
+        copy.wait()
 
 
 VMEM_SPEC = pl.BlockSpec(memory_space=pltpu.VMEM)
@@ -455,32 +483,40 @@
 
 def on_device(tokens, attn_gain, mlp_gain, project_in, project_out, gate_up, project_down, kv_cache, lengths, owners, cache_start):
     shape = jax.ShapeDtypeStruct
-    hidden_states, lse, kv_updated = pl.pallas_call(
+    results = (shape((BLK, D), BF), shape((2, REQ), F32), shape((2, ROWS, 128), BF))
+    held = pl.pallas_call(
         layer_kernel,
-        out_shape=(shape((BLK, D), BF), shape((2, REQ), F32), shape((2, ROWS, 128), BF)),
+        out_shape=results,
         in_specs=[ANY_SPEC] * 11,
         out_specs=(VMEM_SPEC, VMEM_SPEC, ANY_SPEC),
         scratch_shapes=[
             pltpu.VMEM((BLK, D), BF), pltpu.VMEM((16, 128), BF), pltpu.VMEM((16, 128), BF), pltpu.VMEM((3, 32, 128), I32),
-            pltpu.VMEM((D, 384), BF), pltpu.VMEM((128, D), BF), pltpu.VMEM((2, D, FFL), BF), pltpu.VMEM((FFL, D), BF),
+            pltpu.VMEM((D, 384), BF), pltpu.VMEM((2, 128, D), BF), pltpu.VMEM((2, 2, D, FFL), BF), pltpu.VMEM((2, FFL, D), BF),
             pltpu.VMEM((2, ROWS, 128), BF),
-            pltpu.VMEM((2, 2, REQ, HALF), BF), pltpu.VMEM((REQ, 384), BF), pltpu.VMEM((SLOTS, 384), BF),
+            pltpu.VMEM((2, REQ, HALF), BF), pltpu.VMEM((2, 128, HALF), BF), pltpu.VMEM((REQ, 384), BF), pltpu.VMEM((SLOTS, 384), BF),
             pltpu.VMEM((NDP * BLK, 384), BF), pltpu.VMEM((SLOTS, REQ), BF), pltpu.VMEM((REQ, SLOTS), BF),
             pltpu.VMEM((SLOTS, 128), F32), pltpu.VMEM((SLOTS, 128), F32), pltpu.VMEM((8, SLOTS), F32),
             pltpu.VMEM((512, 128), BF), pltpu.VMEM((512, 128), F32), pltpu.VMEM((512, 256), F32),
             pltpu.VMEM((HOME, 256), BF), pltpu.VMEM((NDP * BLK, 256), BF), pltpu.VMEM((NDP * BLK, 256), BF),
-            pltpu.VMEM((SLOTS, 256), BF), pltpu.VMEM((REQ, 128), BF), pltpu.VMEM((REQ, FFL), BF), pltpu.VMEM((BLK, D), BF),
-            pltpu.VMEM((2, 2, 128, HALF), BF), pltpu.VMEM((2, 2, 128, HALF), BF), pltpu.VMEM((2, 128, HALF), F32),
-            pltpu.VMEM((2, 2, 7, BLK, HALF), BF), pltpu.VMEM((2, 2, 7, BLK, HALF), BF),
-            DMA((2, 15)), DMA((2, 15)), DMA((2, 2, 7)), DMA((2, 2, 7)), DMA((2, 16)), DMA((2, 16)),
-            DMA((2, 2, 7)), DMA((2, 2, 7)), DMA((2, 2)), DMA((2, 2)), DMA((13,)), DMA((1,)),
+            pltpu.VMEM((SLOTS, 256), BF), pltpu.VMEM((3, 128, 128), BF), pltpu.VMEM((2, 128, FFL), BF), pltpu.VMEM((BLK, D), BF),
+            pltpu.VMEM((2, 2, 128, HALF), F32), pltpu.VMEM((2, 2, 7, BLK, HALF), BF), pltpu.VMEM((2, 2, 7, BLK, HALF), BF),
+            DMA((2, 15)), DMA((2, 15)), DMA((2, 2, 7)), DMA((2, 2, 7)), DMA((16,)), DMA((16,)),
+            DMA((2, 2, 7)), DMA((2, 2, 7)), DMA((4,)), DMA((4,)), DMA((13,)), DMA((1,)),
         ],
-        compiler_params=pltpu.CompilerParams(collective_id=0, has_side_effects=True, vmem_limit_bytes=56 << 20),
+        compiler_params=pltpu.CompilerParams(collective_id=0, has_side_effects=True, vmem_limit_bytes=54 << 20),
         name="decode_layer",
     )(
         tokens, attn_gain.reshape(16, 128), mlp_gain.reshape(16, 128), lengths.reshape(32, 128), owners.reshape(32, 128),
         cache_start.reshape(32, 128), project_in, project_out, gate_up, project_down, kv_cache,
     )
+    hidden_states, lse, kv_updated = pl.pallas_call(
+        store_kernel,
+        out_shape=results,
+        in_specs=[ANY_SPEC] * 3,
+        out_specs=(ANY_SPEC,) * 3,
+        scratch_shapes=[DMA((10,))],
+        name="store_results",
+    )(*held)
     return hidden_states, lse.T, kv_updated
 
 

time: 95 us -> 139 us (1.46)
  Pallas kernels: 88.5 us -> 138 us
  local copies, waits for them, and re-layouts: 5.76 us -> 0 us
    pallas_call x1 -> x2, Pallas kernels: 88.5 us -> 138 us  [the longest x1 71 us: on_device(): pl.pallas_call(layer_kernel, out_shape=results, in_specs=[ANY_SPEC] * 11,...]
    unnamed x3 -> x0, local copies, waits for them, and re-layouts: 5.76 us -> none
where the time goes in v3:
time: 139 us; the launch traced here: 138 us
  Pallas kernels  138 us (99%)
    pallas_call x1, Pallas kernels, on_device(): pl.pallas_call(layer_kernel, out_shape=results, in_specs=[ANY_SPEC] * 11,...  71 us
    pallas_call x1, Pallas kernels, on_device(): pl.pallas_call(store_kernel, out_shape=results, in_specs=[ANY_SPEC] * 3,...  66.8 us

profile of v3, /device:TPU:32, one launch (start us, length us, event | category | flops | bytes accessed | tf_op | source)
XLA Modules:
  0.0 138.5 jit_solution(1746246818354368449)
XLA Ops:
  0.6 71.0 %decode_layer.1 = (bf16[16,2048]{1,0:T(8,128)(2,1)}, f32[2,256]{1,0:T(2,128)}, bf16[2,4096,128]{2,1,0:T(8,128)(2,1)}) custom-call(bf16[16,2048]{1,0:T(8,128)(2,1)} %tokens_hbm.1, bf16[16,128]{1,0:T(8,128)(2,1)} %bitcast.9, bf16[16,128]{1,0:T(8,128)(2,1)} %bitcast.10, s32[32,128]{1,0:T(8,128)} %bitcast.6, s32[32,128]{1,0:T(8,128)} %bitcast.7, ...), custom_call_target="tpu_custom_call" | custom-call | tf_op jit(solution)/shard_map/decode_layer/pallas_call | solution.py:487
  71.7 66.8 %store_results.1 = (bf16[16,2048]{1,0:T(8,128)(2,1)}, f32[2,256]{1,0:T(2,128)}, bf16[2,4096,128]{2,1,0:T(8,128)(2,1)}) custom-call(bf16[16,2048]{1,0:T(8,128)(2,1)} %get-tuple-element.9.hidden, f32[2,256]{1,0:T(2,128)} %get-tuple-element.10.lse, bf16[2,4096,128]{2,1,0:T(8,128)(2,1)} %get-tuple-element.11.cache), custom_call_target="tpu_custom_call" | custom-call | tf_op jit(solution)/shard_map/store_results/pallas_call | solution.py:512

commit v4 on v3

--- a/solution.py
+++ b/solution.py
@@ -31,6 +31,12 @@
 PBLK = 1024
 
 
+FAR_FIRST = sorted(
+    [(dx, dy) for dx in range(4) for dy in range(4) if (dx, dy) != (0, 0)],
+    key=lambda at: -(min(at[0], 4 - at[0]) + min(at[1], 4 - at[1])),
+)
+
+
 class Place:
     def __init__(self):
         self.d = lax.axis_index("dp")
@@ -42,14 +48,14 @@
     def along_z(self, offset):
         return (self.d, ((self.z + NZ + offset) % NZ) * 2 + self.c)
 
-    def dp_peer(self, offset):
-        return (self.d + offset) % NDP
+    def dp_peer(self, dx, dy):
+        return ((self.d // 4 + dx) % 4) * 4 + (self.d % 4 + dy) % 4
 
 
 def greet(me):
     barrier = pltpu.get_barrier_semaphore()
     targets = [me.along_z(k) for k in (1, -1, 2, -2)] + [me.sib]
-    targets += [(me.dp_peer(i), me.t) for i in range(1, NDP)]
+    targets += [(me.dp_peer(dx, dy), me.t) for dx, dy in FAR_FIRST]
     for target in targets:
         pl.semaphore_signal(barrier, inc=1, device_id=target, device_id_type=MESH)
     return lambda: pl.semaphore_wait(barrier, len(targets))
@@ -178,12 +184,12 @@
 
 def exchange_dp(me, source, landing, send, recv):
     copies = []
-    for i in range(1, NDP):
-        peer = me.dp_peer(i)
+    for i, (dx, dy) in enumerate(FAR_FIRST):
+        peer = me.dp_peer(dx, dy)
         copy = pltpu.make_async_remote_copy(
             src_ref=source.at[pl.ds(pl.multiple_of(peer * BLK, BLK), BLK), :],
             dst_ref=landing.at[pl.ds(pl.multiple_of(me.d * BLK, BLK), BLK), :],
-            send_sem=send.at[i - 1], recv_sem=recv.at[i - 1],
+            send_sem=send.at[i], recv_sem=recv.at[i],
             device_id=(peer, me.t), device_id_type=MESH,
         )
         copy.start()
@@ -199,12 +205,12 @@
 
 def layer_kernel(
     tokens_hbm, attn_gain_hbm, mlp_gain_hbm, lengths_hbm, owners_hbm, starts_hbm, w_hbm, wo_hbm, gu_hbm, wd_hbm, cache_hbm,
-    hidden_out, lse_out, cache_out,
-    tokens, attn_gain, mlp_gain, ints, w, wo, gu, wd, cache,
+    hidden_out, lse_out, cache,
+    tokens, attn_gain, mlp_gain, ints, w, wo, gu, wd,
     gathered, gathered_mlp, packed, compact, outgoing, sel, scat, begin_ref, end_ref, end_row,
     q2, top_ref, out_ref, ret_home, ret_away, landing, slots, attended, inner, resid_keep,
     own, ring_out, ring_in,
-    dp_send, dp_recv, ag_send, ag_recv, ag_sib_send, ag_sib_recv, rs_send, rs_recv, core_send, core_recv, load_sem, store_sem,
+    dp_send, dp_recv, ag_send, ag_recv, ag_sib_send, ag_sib_recv, rs_send, rs_recv, core_send, core_recv, load_sem,
 ):
     me = Place()
     pairs = [
@@ -324,7 +330,6 @@
     outgoing[...] = jnp.dot(sel[HOME:, :], packed[...], preferred_element_type=F32).astype(BF)
     sent = exchange_dp(me, outgoing, compact.at[pl.ds(HOME, NDP * BLK), :], dp_send.at[0], dp_recv.at[0])
     compact[:HOME, :] = jnp.dot(sel[:HOME, :], packed[...], preferred_element_type=F32).astype(BF)
-    shared = [to_core(wo_hbm, wo.at[1], 0), to_core(gu_hbm, gu.at[1], 1), to_core(wd_hbm, wd.at[1], 2)]
     loads[8].wait()
 
     def attend(first, count, ret):
@@ -375,6 +380,7 @@
     drain_gather()
     for copy in sent:
         copy.wait_recv()
+    shared = [to_core(wo_hbm, wo.at[1], 0), to_core(gu_hbm, gu.at[1], 1), to_core(wd_hbm, wd.at[1], 2)]
     attend(HOME, NDP * BLK, ret_away)
     back = exchange_dp(me, ret_away, landing, dp_send.at[1], dp_recv.at[1])
 
@@ -389,8 +395,6 @@
         cache[0, span, :] = jnp.where(hit, fresh[:, 0:128], cache[0, span, :].astype(F32)).astype(BF)
         cache[1, span, :] = jnp.where(hit, fresh[:, 128:256], cache[1, span, :].astype(F32)).astype(BF)
 
-    store = pltpu.make_async_copy(cache, cache_out, store_sem.at[0])
-    store.start()
     slots[:HOME, :] = ret_home[...]
     loads[9].wait()
     for copy in back:
@@ -461,14 +465,10 @@
     for copy in shared:
         copy.wait_send()
     swapped.wait_send()
-    store.wait()
 
 
 def store_kernel(hidden, lse, cache, hidden_out, lse_out, cache_out, sems):
-    pairs = [(hidden, hidden_out), (lse, lse_out)]
-    for part in range(8):
-        span = pl.ds(part % 4 * (ROWS // 4), ROWS // 4)
-        pairs.append((cache.at[part // 4, span], cache_out.at[part // 4, span]))
+    pairs = [(cache.at[0], cache_out.at[0]), (cache.at[1], cache_out.at[1]), (hidden, hidden_out), (lse, lse_out)]
     copies = [pltpu.make_async_copy(src, dst, sems.at[i]) for i, (src, dst) in enumerate(pairs)]
     for copy in copies:
         copy.start()
@@ -486,13 +486,12 @@
     results = (shape((BLK, D), BF), shape((2, REQ), F32), shape((2, ROWS, 128), BF))
     held = pl.pallas_call(
         layer_kernel,
-        out_shape=results,
+        out_shape=(pltpu.VMEM((BLK, D), BF), pltpu.VMEM((2, REQ), F32), pltpu.VMEM((2, ROWS, 128), BF)),
         in_specs=[ANY_SPEC] * 11,
-        out_specs=(VMEM_SPEC, VMEM_SPEC, ANY_SPEC),
+        out_specs=(VMEM_SPEC,) * 3,
         scratch_shapes=[
             pltpu.VMEM((BLK, D), BF), pltpu.VMEM((16, 128), BF), pltpu.VMEM((16, 128), BF), pltpu.VMEM((3, 32, 128), I32),
             pltpu.VMEM((D, 384), BF), pltpu.VMEM((2, 128, D), BF), pltpu.VMEM((2, 2, D, FFL), BF), pltpu.VMEM((2, FFL, D), BF),
-            pltpu.VMEM((2, ROWS, 128), BF),
             pltpu.VMEM((2, REQ, HALF), BF), pltpu.VMEM((2, 128, HALF), BF), pltpu.VMEM((REQ, 384), BF), pltpu.VMEM((SLOTS, 384), BF),
             pltpu.VMEM((NDP * BLK, 384), BF), pltpu.VMEM((SLOTS, REQ), BF), pltpu.VMEM((REQ, SLOTS), BF),
             pltpu.VMEM((SLOTS, 128), F32), pltpu.VMEM((SLOTS, 128), F32), pltpu.VMEM((8, SLOTS), F32),
@@ -501,7 +500,7 @@
             pltpu.VMEM((SLOTS, 256), BF), pltpu.VMEM((3, 128, 128), BF), pltpu.VMEM((2, 128, FFL), BF), pltpu.VMEM((BLK, D), BF),
             pltpu.VMEM((2, 2, 128, HALF), F32), pltpu.VMEM((2, 2, 7, BLK, HALF), BF), pltpu.VMEM((2, 2, 7, BLK, HALF), BF),
             DMA((2, 15)), DMA((2, 15)), DMA((2, 2, 7)), DMA((2, 2, 7)), DMA((16,)), DMA((16,)),
-            DMA((2, 2, 7)), DMA((2, 2, 7)), DMA((4,)), DMA((4,)), DMA((13,)), DMA((1,)),
+            DMA((2, 2, 7)), DMA((2, 2, 7)), DMA((4,)), DMA((4,)), DMA((13,)),
         ],
         compiler_params=pltpu.CompilerParams(collective_id=0, has_side_effects=True, vmem_limit_bytes=54 << 20),
         name="decode_layer",
@@ -512,11 +511,11 @@
     hidden_states, lse, kv_updated = pl.pallas_call(
         store_kernel,
         out_shape=results,
-        in_specs=[ANY_SPEC] * 3,
+        in_specs=[VMEM_SPEC] * 3,
         out_specs=(ANY_SPEC,) * 3,
-        scratch_shapes=[DMA((10,))],
+        scratch_shapes=[DMA((4,))],
         name="store_results",
-    )(*held)
+    )(*(pltpu.with_memory_space_constraint(value, pltpu.VMEM) for value in held))
     return hidden_states, lse.T, kv_updated
 
 

time: 139 us -> 71.9 us (0.52)
  Pallas kernels: 138 us -> 71.2 us
    pallas_call x2, Pallas kernels: 138 us -> 71.2 us  [the longest x1 69.8 us: on_device(): pl.pallas_call(layer_kernel, out_shape=(pltpu.VMEM((BLK, D), BF), pltpu.V...]
where the time goes in v4:
time: 71.9 us; the launch traced here: 71.8 us
  Pallas kernels  71.2 us (99%)
    pallas_call x1, Pallas kernels, on_device(): pl.pallas_call(layer_kernel, out_shape=(pltpu.VMEM((BLK, D), BF), pltpu.V...  69.8 us

profile of v4, /device:TPU:32, one launch (start us, length us, event | category | flops | bytes accessed | tf_op | source)
XLA Modules:
  0.0 71.8 jit_solution(243622711995766180)
XLA Ops:
  0.6 69.8 %decode_layer.1 = (bf16[16,2048]{1,0:T(8,128)(2,1)S(1)}, f32[2,256]{1,0:T(2,128)S(1)}, bf16[2,4096,128]{2,1,0:T(8,128)(2,1)S(1)}) custom-call(bf16[16,2048]{1,0:T(8,128)(2,1)} %tokens_hbm.1, bf16[16,128]{1,0:T(8,128)(2,1)} %bitcast.9, bf16[16,128]{1,0:T(8,128)(2,1)} %bitcast.10, s32[32,128]{1,0:T(8,128)} %bitcast.6, s32[32,128]{1,0:T(8,128)} %bitcast.7, ...), custom_call_target="tpu_custom_call" | custom-call | tf_op jit(solution)/shard_map/decode_layer/pallas_call | solution.py:487
  70.4 1.4 %store_results.1 = (bf16[16,2048]{1,0:T(8,128)(2,1)}, f32[2,256]{1,0:T(2,128)}, bf16[2,4096,128]{2,1,0:T(8,128)(2,1)}) custom-call(bf16[16,2048]{1,0:T(8,128)(2,1)S(1)} %get-tuple-element.9.hidden, f32[2,256]{1,0:T(2,128)S(1)} %get-tuple-element.10.lse, bf16[2,4096,128]{2,1,0:T(8,128)(2,1)S(1)} %get-tuple-element.11.cache), custom_call_target="tpu_custom_call" | custom-call | tf_op jit(solution)/shard_map/store_results/pallas_call | solution.py:511

commit v5 on v4

--- a/solution.py
+++ b/solution.py
@@ -28,7 +28,10 @@
 SLOTS = HOME + NDP * BLK
 ROWS = 4096
 FFL = 512
-PBLK = 1024
+PBLK = 2048
+SPAN = 512
+CAP = 9
+BATCH = 80
 
 
 FAR_FIRST = sorted(
@@ -124,6 +127,7 @@
         for index in (0, 1, 2, 3, 4, 5, 6):
             for way in range(2):
                 arrive(way, index if index in (2, 3, 6) else index ^ way)
+    def settle():
         for copy in sib_copies:
             copy.wait_recv()
 
@@ -131,7 +135,7 @@
         for copy in started + sib_copies:
             copy.wait_send()
 
-    return begin, finish, drain
+    return begin, finish, settle, drain
 
 
 def reduce_z(me, product, own, out, landed, send, recv):
@@ -207,8 +211,9 @@
     tokens_hbm, attn_gain_hbm, mlp_gain_hbm, lengths_hbm, owners_hbm, starts_hbm, w_hbm, wo_hbm, gu_hbm, wd_hbm, cache_hbm,
     hidden_out, lse_out, cache,
     tokens, attn_gain, mlp_gain, ints, w, wo, gu, wd,
-    gathered, gathered_mlp, packed, compact, outgoing, sel, scat, begin_ref, end_ref, end_row,
-    q2, top_ref, out_ref, ret_home, ret_away, landing, slots, attended, inner, resid_keep,
+    gathered, gathered_mlp, packed, compact, outgoing, sel, route, scat, begin_ref, end_ref, end_row,
+    pick, begin_away, end_away, away_ref, cos_ref, sin_ref,
+    q2, score_ref, ret_away, landing, slots, attended, inner, resid_keep,
     own, ring_out, ring_in,
     dp_send, dp_recv, ag_send, ag_recv, ag_sib_send, ag_sib_recv, rs_send, rs_recv, core_send, core_recv, load_sem,
 ):
@@ -229,12 +234,12 @@
         return jnp.concatenate([ref[i : i + 1, :].astype(F32) for i in range(16)], axis=1)
 
     normed = scaled_norm(tokens[...].astype(F32), gain_row(attn_gain))
-    row_of = lambda zz, cc: (zz * 2 + cc) * BLK
+    row_of = lambda zz, cc: cc * 128 + zz * BLK
     my_rows = pl.ds(pl.multiple_of(row_of(me.z, me.c), BLK), BLK)
     for half in range(2):
         gathered[half, my_rows, :] = normed[:, half * HALF : (half + 1) * HALF]
     wait_all()
-    begin, finish, drain_gather = gather_z(
+    begin, finish, settle, drain_gather = gather_z(
         me, gathered, row_of, ag_send.at[0], ag_recv.at[0], ag_sib_send, ag_sib_recv
     )
     begin()
@@ -264,7 +269,10 @@
     sel[...] = jnp.where(chosen, 1.0, 0.0).astype(BF)
     request = iota((REQ, REQ), 0)
     natural = ((request >> 4) & 7) * 32 + (request >> 7) * 16 + (request & 15)
-    place_col = column_of(place, natural == iota((REQ, REQ), 1))
+    reorder = natural == iota((REQ, REQ), 1)
+    place_col = column_of(place, reorder)
+    place_row = jnp.sum(jnp.where(request == iota((REQ, REQ), 1), place_col, 0.0), axis=0, keepdims=True)
+    route[...] = jnp.where(iota((SLOTS, REQ), 0).astype(F32) == place_row, 1.0, 0.0).astype(BF)
     scat[...] = jnp.where(iota((REQ, SLOTS), 1).astype(F32) == place_col, 1.0, 0.0).astype(BF)
 
     def spread(rows16):
@@ -283,12 +291,27 @@
     finish_col = jnp.concatenate(
         [column_of(start_row + len_row + 1.0, hits_home), column_of(spread(finish_all) + 1.0, hits_in)], axis=0
     ) - 1.0
-    begin_ref[...] = jnp.broadcast_to(begin_col, (SLOTS, 128))
-    end_ref[...] = jnp.broadcast_to(finish_col, (SLOTS, 128))
+    begin_ref[...] = jnp.broadcast_to(begin_col[:HOME], (HOME, 128))
+    end_ref[...] = jnp.broadcast_to(finish_col[:HOME], (HOME, 128))
     eye = iota((SLOTS, SLOTS), 0) == iota((SLOTS, SLOTS), 1)
-    end_row[...] = jnp.broadcast_to(jnp.sum(jnp.where(eye, finish_col, 0.0), axis=0, keepdims=True), (8, SLOTS))
-
-    len_col = column_of(len_row, iota((REQ, REQ), 0) == iota((REQ, REQ), 1))
+    finish_row = jnp.sum(jnp.where(eye, finish_col, 0.0), axis=0, keepdims=True)
+    begin_row = jnp.sum(jnp.where(eye, begin_col, 0.0), axis=0, keepdims=True)
+    end_row[...] = jnp.broadcast_to(finish_row, (8, SLOTS))
+    index = iota((2 * BATCH, 1), 0).astype(F32)
+    second = index >= BATCH
+    within = jnp.where(second, index - BATCH, index)
+    nth = jnp.floor((within + 0.5) * (1.0 / CAP))
+    source = jnp.full((2 * BATCH, 1), -1000.0, F32)
+    for k, (dx, dy) in enumerate(FAR_FIRST):
+        at = (nth == k % 8) & (second if k >= 8 else jnp.logical_not(second))
+        source = jnp.where(at, (me.dp_peer(dx, dy) * BLK).astype(F32), source)
+    source = source + within - nth * CAP
+    picked = iota((2 * BATCH, NDP * BLK), 1).astype(F32) == source
+    pick[...] = jnp.where(picked, 1.0, 0.0).astype(BF)
+    begin_away[...] = jnp.broadcast_to(column_of(begin_row[:, HOME:] + 1.0, picked) - 1.0, (2 * BATCH, 128))
+    end_away[...] = jnp.broadcast_to(column_of(finish_row[:, HOME:] + 1.0, picked) - 1.0, (2 * BATCH, 128))
+
+    len_col = column_of(len_row, reorder)
     lane = iota((1, 128), 1) & (HD // 2 - 1)
     freqs = jnp.exp(lane.astype(F32) * np.float32(-np.log(ROPE_BASE) / (HD // 2)))
     angle = len_col * freqs
@@ -301,9 +324,8 @@
         -1 / 2 + x2 * (1 / 24 + x2 * (-1 / 720 + x2 * (1 / 40320 + x2 * (-1 / 3628800 + x2 / 479001600))))
     )
     sine = 2.0 * sin_half * cos_half
-    cosine = 1.0 - 2.0 * sin_half * sin_half
-    low_half = (iota((REQ, 128), 1) & (HD - 1)) < HD // 2
-    signed = jnp.where(low_half, -sine, sine)
+    cos_ref[...] = 1.0 - 2.0 * sin_half * sin_half
+    sin_ref[...] = jnp.where((iota((REQ, 128), 1) & (HD - 1)) < HD // 2, -sine, sine)
 
     finish()
 
@@ -317,72 +339,92 @@
 
     for copy in loads[5:8]:
         copy.wait()
-    projected = jnp.dot(gathered[0], w[:HALF], preferred_element_type=F32)
-    projected = projected + jnp.dot(gathered[1], w[HALF:], preferred_element_type=F32)
-
-    def turned(values):
-        partner = jnp.where(low_half, pltpu.roll(values, 96, 1), pltpu.roll(values, 32, 1))
-        return (values * cosine + partner * signed).astype(BF)
-
-    packed[:, 0:128] = turned(projected[:, 0:128])
-    packed[:, 128:256] = turned(projected[:, 128:256])
-    packed[:, 256:384] = projected[:, 256:384].astype(BF)
-    outgoing[...] = jnp.dot(sel[HOME:, :], packed[...], preferred_element_type=F32).astype(BF)
+    low_half = (iota((128, 128), 1) & (HD - 1)) < HD // 2
+
+    def project(core):
+        rows = pl.ds(pl.multiple_of(core * 128, 128), 128)
+        projected = jnp.dot(gathered[0, rows, :], w[:HALF], preferred_element_type=F32)
+        projected = projected + jnp.dot(gathered[1, rows, :], w[HALF:], preferred_element_type=F32)
+        for m in range(2):
+            values = projected[:, m * 128 : (m + 1) * 128]
+            partner = jnp.where(low_half, pltpu.roll(values, 96, 1), pltpu.roll(values, 32, 1))
+            packed[rows, m * 128 : (m + 1) * 128] = (values * cos_ref[rows, :] + partner * sin_ref[rows, :]).astype(BF)
+        packed[rows, 256:384] = projected[:, 256:384].astype(BF)
+
+    project(me.c)
+    settle()
+    project(1 - me.c)
+    outgoing[...] = jnp.dot(route[HOME:, :], packed[...], preferred_element_type=F32).astype(BF)
     sent = exchange_dp(me, outgoing, compact.at[pl.ds(HOME, NDP * BLK), :], dp_send.at[0], dp_recv.at[0])
-    compact[:HOME, :] = jnp.dot(sel[:HOME, :], packed[...], preferred_element_type=F32).astype(BF)
+    compact[:HOME, :] = jnp.dot(route[:HOME, :], packed[...], preferred_element_type=F32).astype(BF)
     loads[8].wait()
 
-    def attend(first, count, ret):
+    def attend(operand, begins, ends, count):
         low_lanes = iota((count, 128), 1) < HD
-        rows = pl.ds(first, count)
-        q = compact[rows, 0:128].astype(F32) * (1.0 / 8.0)
-        k = compact[rows, 128:256].astype(F32)
-        v = compact[rows, 256:384].astype(F32)
+        q = operand[:count, 0:128].astype(F32) * (1.0 / 8.0)
+        k = operand[:count, 128:256].astype(F32)
+        v = operand[:count, 256:384].astype(F32)
+        spans = [pl.ds(head * count, count) for head in range(2)]
+        chunks = [pl.ds(first, SPAN) for first in range(0, ROWS, SPAN)]
+        own_score, top = [], []
         for head in range(2):
-            keep = low_lanes if head == 0 else jnp.logical_not(low_lanes)
-            qh = jnp.where(keep, q, 0.0)
-            own_rows = pl.ds(head * count, count)
-            q2[own_rows, :] = qh.astype(BF)
-            top_ref[own_rows, :] = jnp.broadcast_to(jnp.sum(qh * k, axis=1, keepdims=True), (count, 128))
-            out_ref[own_rows, 0:128] = v
-            out_ref[own_rows, 128:256] = jnp.ones((count, 128), F32)
-
-        @pl.loop(0, ROWS // PBLK)
-        def _(block):
-            base = pl.multiple_of(block * PBLK, PBLK)
-            keys = cache[0, pl.ds(base, PBLK), :]
-            values = jnp.concatenate([cache[1, pl.ds(base, PBLK), :], jnp.ones((PBLK, 128), BF)], axis=1)
-            across = (iota((1, PBLK), 1) + base).astype(F32)
-            live = (across >= begin_ref[rows, 0:1]) & (across < end_ref[rows, 0:1])
+            qh = jnp.where(low_lanes if head == 0 else jnp.logical_not(low_lanes), q, 0.0)
+            q2[spans[head], :] = qh.astype(BF)
+            own_score.append(jnp.sum(qh * k, axis=1, keepdims=True))
+            top.append(jnp.full((count, 128), LOW, F32))
+        for chunk in chunks:
+            across = (iota((1, SPAN), 1) + chunk.start).astype(F32)
+            live = (across >= begins[:count, 0:1]) & (across < ends[:count, 0:1])
             for head in range(2):
-                own_rows = pl.ds(head * count, count)
-                scores = lax.dot_general(q2[own_rows, :], keys, (((1,), (1,)), ((), ())), preferred_element_type=F32)
+                scores = lax.dot_general(
+                    q2[spans[head], :], cache[0, chunk, :], (((1,), (1,)), ((), ())), preferred_element_type=F32
+                )
                 scores = jnp.where(live, scores, LOW)
-                old_top = top_ref[own_rows, 0:1]
-                top = jnp.maximum(old_top, jnp.max(scores, axis=1, keepdims=True))
-                weights = jnp.exp(scores - top).astype(BF)
-                added = jnp.dot(weights, values, preferred_element_type=F32)
-                out_ref[own_rows, :] = out_ref[own_rows, :] * jnp.exp(old_top - top) + added
-                top_ref[own_rows, :] = jnp.broadcast_to(top, (count, 128))
-
-        first_rows, second_rows = pl.ds(0, count), pl.ds(count, count)
-        upper = jnp.where(low_lanes, out_ref[first_rows, 0:128], out_ref[second_rows, 0:128])
-        lower = jnp.where(low_lanes, out_ref[first_rows, 128:256], out_ref[second_rows, 128:256])
-        ret[:, 0:128] = (upper / lower).astype(BF)
-        lse = [top_ref[r, :] + jnp.log(out_ref[r, 128:256]) for r in (first_rows, second_rows)]
+                score_ref[spans[head], chunk] = scores
+                for first in range(0, SPAN, 128):
+                    top[head] = jnp.maximum(top[head], scores[:, first : first + 128])
+        out, lse = [], []
+        for head in range(2):
+            peak = jnp.maximum(own_score[head], jnp.max(top[head], axis=1, keepdims=True))
+            own_weight = jnp.exp(own_score[head] - peak)
+            summed = jnp.concatenate([own_weight * v, jnp.broadcast_to(own_weight, (count, 128))], axis=1)
+            for chunk in chunks:
+                weights = jnp.exp(score_ref[spans[head], chunk] - peak).astype(BF)
+                values = jnp.concatenate([cache[1, chunk, :], jnp.ones((SPAN, 128), BF)], axis=1)
+                summed = summed + jnp.dot(weights, values, preferred_element_type=F32)
+            out.append(summed[:, 0:128] / summed[:, 128:256])
+            lse.append(peak + jnp.log(summed[:, 128:256]))
         high = [value.astype(BF).astype(F32) for value in lse]
-        low = [a - b for a, b in zip(lse, high)]
+        low = [x - y for x, y in zip(lse, high)]
         lane = iota((count, 128), 1)
         tail = jnp.where(lane == 0, high[0], jnp.where(lane == 1, low[0], jnp.where(lane == 2, high[1], low[1])))
-        ret[:, 128:256] = tail.astype(BF)
-
-    attend(0, HOME, ret_home)
+        return jnp.concatenate([jnp.where(low_lanes, out[0], out[1]).astype(BF), tail.astype(BF)], axis=1)
+
+    slots[:HOME, :] = attend(compact, begin_ref, end_ref, HOME)
     drain_gather()
     for copy in sent:
         copy.wait_recv()
-    shared = [to_core(wo_hbm, wo.at[1], 0), to_core(gu_hbm, gu.at[1], 1), to_core(wd_hbm, wd.at[1], 2)]
-    attend(HOME, NDP * BLK, ret_away)
-    back = exchange_dp(me, ret_away, landing, dp_send.at[1], dp_recv.at[1])
+    shared = [to_core(wo_hbm, wo.at[1], 0)]
+    away_ref[...] = jnp.dot(pick[...], compact[HOME:, :], preferred_element_type=F32).astype(BF)
+    line = iota((8 * BLK, BATCH), 0)
+    unpick = ((line >> 4) * CAP + (line & 15) == iota((8 * BLK, BATCH), 1)) & ((line & 15) < CAP)
+    unpick = jnp.where(unpick, 1.0, 0.0).astype(BF)
+    landing[pl.ds(pl.multiple_of(me.d * BLK, BLK), BLK), :] = jnp.zeros((BLK, 256), BF)
+    back = []
+    found = attend(away_ref, begin_away, end_away, 2 * BATCH)
+    for batch in range(2):
+        ret_away[batch] = jnp.dot(
+            unpick, found[batch * BATCH : (batch + 1) * BATCH], preferred_element_type=F32
+        ).astype(BF)
+        for k in range(batch * 8, min(batch * 8 + 8, NDP - 1)):
+            copy = pltpu.make_async_remote_copy(
+                src_ref=ret_away.at[batch, pl.ds(k % 8 * BLK, BLK), :],
+                dst_ref=landing.at[pl.ds(pl.multiple_of(me.d * BLK, BLK), BLK), :],
+                send_sem=dp_send.at[1, k], recv_sem=dp_recv.at[1, k],
+                device_id=(me.dp_peer(*FAR_FIRST[k]), me.t), device_id_type=MESH,
+            )
+            copy.start()
+            back.append(copy)
 
     @pl.loop(0, ROWS // PBLK)
     def _(block):
@@ -395,7 +437,6 @@
         cache[0, span, :] = jnp.where(hit, fresh[:, 0:128], cache[0, span, :].astype(F32)).astype(BF)
         cache[1, span, :] = jnp.where(hit, fresh[:, 128:256], cache[1, span, :].astype(F32)).astype(BF)
 
-    slots[:HOME, :] = ret_home[...]
     loads[9].wait()
     for copy in back:
         copy.wait_recv()
@@ -408,13 +449,15 @@
     attended[2] = assemble(1 - me.c)
     swapped = to_core(attended.at[2], attended.at[1], 3)
     attended[0] = assemble(me.c)
+    for half in range(2):
+        own[0, half] = jnp.dot(attended[0], wo[0, :, half * HALF : (half + 1) * HALF], preferred_element_type=F32)
     shared[0].wait_recv()
     swapped.wait_recv()
+    shared += [to_core(gu_hbm, gu.at[1], 1), to_core(wd_hbm, wd.at[1], 2)]
 
     def out_product(half):
         columns = pl.ds(half * HALF, HALF)
-        value = jnp.dot(attended[0], wo[0, :, columns], preferred_element_type=F32)
-        return value + jnp.dot(attended[1], wo[1, :, columns], preferred_element_type=F32)
+        return own[0, half] + jnp.dot(attended[1], wo[1, :, columns], preferred_element_type=F32)
 
     total, drain_first = reduce_z(
         me, out_product, own.at[0], ring_out.at[0], ring_in.at[0], rs_send.at[0], rs_recv.at[0]
@@ -427,7 +470,7 @@
     my_rows = pl.ds(pl.multiple_of(me.z * BLK, BLK), BLK)
     for half in range(2):
         gathered_mlp[half, my_rows, :] = normed[:, half * HALF : (half + 1) * HALF]
-    begin, finish_mlp, drain_mlp = gather_z(me, gathered_mlp, row_of_chip, ag_send.at[1], ag_recv.at[1])
+    begin, finish_mlp, _, drain_mlp = gather_z(me, gathered_mlp, row_of_chip, ag_send.at[1], ag_recv.at[1])
     begin()
     spread_sel = sel[...].astype(F32)
     tail = slots[:, 128:256].astype(F32)
@@ -493,10 +536,12 @@
             pltpu.VMEM((BLK, D), BF), pltpu.VMEM((16, 128), BF), pltpu.VMEM((16, 128), BF), pltpu.VMEM((3, 32, 128), I32),
             pltpu.VMEM((D, 384), BF), pltpu.VMEM((2, 128, D), BF), pltpu.VMEM((2, 2, D, FFL), BF), pltpu.VMEM((2, FFL, D), BF),
             pltpu.VMEM((2, REQ, HALF), BF), pltpu.VMEM((2, 128, HALF), BF), pltpu.VMEM((REQ, 384), BF), pltpu.VMEM((SLOTS, 384), BF),
-            pltpu.VMEM((NDP * BLK, 384), BF), pltpu.VMEM((SLOTS, REQ), BF), pltpu.VMEM((REQ, SLOTS), BF),
-            pltpu.VMEM((SLOTS, 128), F32), pltpu.VMEM((SLOTS, 128), F32), pltpu.VMEM((8, SLOTS), F32),
-            pltpu.VMEM((512, 128), BF), pltpu.VMEM((512, 128), F32), pltpu.VMEM((512, 256), F32),
-            pltpu.VMEM((HOME, 256), BF), pltpu.VMEM((NDP * BLK, 256), BF), pltpu.VMEM((NDP * BLK, 256), BF),
+            pltpu.VMEM((NDP * BLK, 384), BF), pltpu.VMEM((SLOTS, REQ), BF), pltpu.VMEM((SLOTS, REQ), BF), pltpu.VMEM((REQ, SLOTS), BF),
+            pltpu.VMEM((HOME, 128), F32), pltpu.VMEM((HOME, 128), F32), pltpu.VMEM((8, SLOTS), F32),
+            pltpu.VMEM((2 * BATCH, NDP * BLK), BF), pltpu.VMEM((2 * BATCH, 128), F32), pltpu.VMEM((2 * BATCH, 128), F32),
+            pltpu.VMEM((2 * BATCH, 384), BF), pltpu.VMEM((REQ, 128), F32), pltpu.VMEM((REQ, 128), F32),
+            pltpu.VMEM((4 * BATCH, 128), BF), pltpu.VMEM((4 * BATCH, ROWS), F32),
+            pltpu.VMEM((2, 8 * BLK, 256), BF), pltpu.VMEM((NDP * BLK, 256), BF),
             pltpu.VMEM((SLOTS, 256), BF), pltpu.VMEM((3, 128, 128), BF), pltpu.VMEM((2, 128, FFL), BF), pltpu.VMEM((BLK, D), BF),
             pltpu.VMEM((2, 2, 128, HALF), F32), pltpu.VMEM((2, 2, 7, BLK, HALF), BF), pltpu.VMEM((2, 2, 7, BLK, HALF), BF),
             DMA((2, 15)), DMA((2, 15)), DMA((2, 2, 7)), DMA((2, 2, 7)), DMA((16,)), DMA((16,)),

time: 71.9 us -> 69.4 us (0.965)
  Pallas kernels: 71.2 us -> 68.4 us
    pallas_call x1, Pallas kernels: 69.8 us -> 67 us  [on_device(): pl.pallas_call(layer_kernel, out_shape=(pltpu.VMEM((BLK, D), BF), pltpu.V...]
where the time goes in v5:
time: 69.4 us; the launch traced here: 69 us
  Pallas kernels  68.4 us (99%)
    pallas_call x1, Pallas kernels, on_device(): pl.pallas_call(layer_kernel, out_shape=(pltpu.VMEM((BLK, D), BF), pltpu.V...  67 us

profile of v5, /device:TPU:32, one launch (start us, length us, event | category | flops | bytes accessed | tf_op | source)
XLA Modules:
  0.0 69.0 jit_solution(8426800940066890105)
XLA Ops:
  0.6 67.0 %decode_layer.1 = (bf16[16,2048]{1,0:T(8,128)(2,1)S(1)}, f32[2,256]{1,0:T(2,128)S(1)}, bf16[2,4096,128]{2,1,0:T(8,128)(2,1)S(1)}) custom-call(bf16[16,2048]{1,0:T(8,128)(2,1)} %tokens_hbm.1, bf16[16,128]{1,0:T(8,128)(2,1)} %bitcast.9, bf16[16,128]{1,0:T(8,128)(2,1)} %bitcast.10, s32[32,128]{1,0:T(8,128)} %bitcast.6, s32[32,128]{1,0:T(8,128)} %bitcast.7, ...), custom_call_target="tpu_custom_call" | custom-call | tf_op jit(solution)/shard_map/decode_layer/pallas_call | solution.py:530
  67.7 1.4 %store_results.1 = (bf16[16,2048]{1,0:T(8,128)(2,1)}, f32[2,256]{1,0:T(2,128)}, bf16[2,4096,128]{2,1,0:T(8,128)(2,1)}) custom-call(bf16[16,2048]{1,0:T(8,128)(2,1)S(1)} %get-tuple-element.9.hidden, f32[2,256]{1,0:T(2,128)S(1)} %get-tuple-element.10.lse, bf16[2,4096,128]{2,1,0:T(8,128)(2,1)S(1)} %get-tuple-element.11.cache), custom_call_target="tpu_custom_call" | custom-call | tf_op jit(solution)/shard_map/store_results/pallas_call | solution.py:556

commit v6 on v5

--- a/solution.py
+++ b/solution.py
@@ -46,7 +46,8 @@
         self.t = lax.axis_index("tensor")
         self.z = self.t // 2
         self.c = self.t % 2
-        self.sib = (self.d, self.t + 1 - 2 * self.c)
+        self.other = self.t + 1 - 2 * self.c
+        self.sib = (self.d, self.other)
 
     def along_z(self, offset):
         return (self.d, ((self.z + NZ + offset) % NZ) * 2 + self.c)
@@ -58,7 +59,7 @@
 def greet(me):
     barrier = pltpu.get_barrier_semaphore()
     targets = [me.along_z(k) for k in (1, -1, 2, -2)] + [me.sib]
-    targets += [(me.dp_peer(dx, dy), me.t) for dx, dy in FAR_FIRST]
+    targets += [(me.dp_peer(dx, dy), t) for dx, dy in FAR_FIRST for t in (me.t, me.other)]
     for target in targets:
         pl.semaphore_signal(barrier, inc=1, device_id=target, device_id_type=MESH)
     return lambda: pl.semaphore_wait(barrier, len(targets))
@@ -211,9 +212,9 @@
     tokens_hbm, attn_gain_hbm, mlp_gain_hbm, lengths_hbm, owners_hbm, starts_hbm, w_hbm, wo_hbm, gu_hbm, wd_hbm, cache_hbm,
     hidden_out, lse_out, cache,
     tokens, attn_gain, mlp_gain, ints, w, wo, gu, wd,
-    gathered, gathered_mlp, packed, compact, outgoing, sel, route, scat, begin_ref, end_ref, end_row,
-    pick, begin_away, end_away, away_ref, cos_ref, sin_ref,
-    q2, score_ref, ret_away, landing, slots, attended, inner, resid_keep,
+    gathered, gathered_mlp, packed, query, fresh_kv, outgoing, sel, route, scat, begin_ref, end_ref, end_row,
+    pick, begin_away, end_away, away_q, away_kv, cos_ref, sin_ref,
+    q2, score_ref, ret_away, slots, tails, attended, inner, resid_keep,
     own, ring_out, ring_in,
     dp_send, dp_recv, ag_send, ag_recv, ag_sib_send, ag_sib_recv, rs_send, rs_recv, core_send, core_recv, load_sem,
 ):
@@ -224,9 +225,11 @@
         (w_hbm.at[2], w.at[:, pl.ds(256, 128)]), (cache_hbm, cache), (wo_hbm, wo.at[0]), (mlp_gain_hbm, mlp_gain), (gu_hbm, gu.at[0]), (wd_hbm, wd.at[0]),
     ]
     loads = [pltpu.make_async_copy(src, dst, load_sem.at[i]) for i, (src, dst) in enumerate(pairs)]
-    for copy in loads:
+    for copy in loads[:2]:
         copy.start()
     wait_all = greet(me)
+    for copy in loads[2:]:
+        copy.start()
     loads[0].wait()
     loads[1].wait()
 
@@ -354,23 +357,25 @@
     project(me.c)
     settle()
     project(1 - me.c)
-    outgoing[...] = jnp.dot(route[HOME:, :], packed[...], preferred_element_type=F32).astype(BF)
-    sent = exchange_dp(me, outgoing, compact.at[pl.ds(HOME, NDP * BLK), :], dp_send.at[0], dp_recv.at[0])
-    compact[:HOME, :] = jnp.dot(route[:HOME, :], packed[...], preferred_element_type=F32).astype(BF)
+    sent = []
+    for lanes, landing, row in ((pl.ds(0, 128), query, 0), (pl.ds(128, 256), fresh_kv, 3)):
+        outgoing[:, lanes] = jnp.dot(route[HOME:, :], packed[:, lanes], preferred_element_type=F32).astype(BF)
+        there = landing.at[pl.ds(HOME, NDP * BLK), :]
+        sent.append(exchange_dp(me, outgoing.at[:, lanes], there, dp_send.at[row], dp_recv.at[row]))
+    home = jnp.dot(route[:HOME, :], packed[...], preferred_element_type=F32).astype(BF)
+    query[:HOME, :] = home[:, 0:128]
+    fresh_kv[:HOME, :] = home[:, 128:384]
     loads[8].wait()
 
-    def attend(operand, begins, ends, count):
+    def attend(queries, pair, begins, ends, count, ready):
         low_lanes = iota((count, 128), 1) < HD
-        q = operand[:count, 0:128].astype(F32) * (1.0 / 8.0)
-        k = operand[:count, 128:256].astype(F32)
-        v = operand[:count, 256:384].astype(F32)
+        q = queries[:count, :].astype(F32) * (1.0 / 8.0)
         spans = [pl.ds(head * count, count) for head in range(2)]
         chunks = [pl.ds(first, SPAN) for first in range(0, ROWS, SPAN)]
-        own_score, top = [], []
+        top = []
         for head in range(2):
             qh = jnp.where(low_lanes if head == 0 else jnp.logical_not(low_lanes), q, 0.0)
             q2[spans[head], :] = qh.astype(BF)
-            own_score.append(jnp.sum(qh * k, axis=1, keepdims=True))
             top.append(jnp.full((count, 128), LOW, F32))
         for chunk in chunks:
             across = (iota((1, SPAN), 1) + chunk.start).astype(F32)
@@ -383,10 +388,14 @@
                 score_ref[spans[head], chunk] = scores
                 for first in range(0, SPAN, 128):
                     top[head] = jnp.maximum(top[head], scores[:, first : first + 128])
+        ready()
+        k = pair[:count, 0:128].astype(F32)
+        v = pair[:count, 128:256].astype(F32)
         out, lse = [], []
         for head in range(2):
-            peak = jnp.maximum(own_score[head], jnp.max(top[head], axis=1, keepdims=True))
-            own_weight = jnp.exp(own_score[head] - peak)
+            own_score = jnp.sum(q2[spans[head], :].astype(F32) * k, axis=1, keepdims=True)
+            peak = jnp.maximum(own_score, jnp.max(top[head], axis=1, keepdims=True))
+            own_weight = jnp.exp(own_score - peak)
             summed = jnp.concatenate([own_weight * v, jnp.broadcast_to(own_weight, (count, 128))], axis=1)
             for chunk in chunks:
                 weights = jnp.exp(score_ref[spans[head], chunk] - peak).astype(BF)
@@ -398,33 +407,50 @@
         low = [x - y for x, y in zip(lse, high)]
         lane = iota((count, 128), 1)
         tail = jnp.where(lane == 0, high[0], jnp.where(lane == 1, low[0], jnp.where(lane == 2, high[1], low[1])))
-        return jnp.concatenate([jnp.where(low_lanes, out[0], out[1]).astype(BF), tail.astype(BF)], axis=1)
-
-    slots[:HOME, :] = attend(compact, begin_ref, end_ref, HOME)
+        return jnp.where(low_lanes, out[0], out[1]).astype(BF), tail.astype(BF)
+
+    slots[0, :HOME, :], tails[:HOME, :] = attend(query, fresh_kv, begin_ref, end_ref, HOME, lambda: None)
     drain_gather()
-    for copy in sent:
+    for copy in sent[0]:
         copy.wait_recv()
+    swapped = to_core(slots.at[0, pl.ds(0, HOME), :], slots.at[1, pl.ds(0, HOME), :], 3)
     shared = [to_core(wo_hbm, wo.at[1], 0)]
-    away_ref[...] = jnp.dot(pick[...], compact[HOME:, :], preferred_element_type=F32).astype(BF)
+    away_q[...] = jnp.dot(pick[...], query[HOME:, :], preferred_element_type=F32).astype(BF)
     line = iota((8 * BLK, BATCH), 0)
     unpick = ((line >> 4) * CAP + (line & 15) == iota((8 * BLK, BATCH), 1)) & ((line & 15) < CAP)
     unpick = jnp.where(unpick, 1.0, 0.0).astype(BF)
-    landing[pl.ds(pl.multiple_of(me.d * BLK, BLK), BLK), :] = jnp.zeros((BLK, 256), BF)
-    back = []
-    found = attend(away_ref, begin_away, end_away, 2 * BATCH)
-    for batch in range(2):
-        ret_away[batch] = jnp.dot(
-            unpick, found[batch * BATCH : (batch + 1) * BATCH], preferred_element_type=F32
-        ).astype(BF)
-        for k in range(batch * 8, min(batch * 8 + 8, NDP - 1)):
+    mine_there = pl.ds(pl.multiple_of(HOME + me.d * BLK, BLK), BLK)
+    tails[mine_there, :] = jnp.zeros((BLK, 128), BF)
+    for which in range(2):
+        slots[which, mine_there, :] = jnp.zeros((BLK, 128), BF)
+
+    def take_kv():
+        for copy in sent[1]:
+            copy.wait_recv()
+        away_kv[...] = jnp.dot(pick[...], fresh_kv[HOME:, :], preferred_element_type=F32).astype(BF)
+
+    found = attend(away_q, away_kv, begin_away, end_away, 2 * BATCH, take_kv)
+
+    def give(part, row, core, landing):
+        copies = []
+        for k in range(NDP - 1):
             copy = pltpu.make_async_remote_copy(
-                src_ref=ret_away.at[batch, pl.ds(k % 8 * BLK, BLK), :],
-                dst_ref=landing.at[pl.ds(pl.multiple_of(me.d * BLK, BLK), BLK), :],
-                send_sem=dp_send.at[1, k], recv_sem=dp_recv.at[1, k],
-                device_id=(me.dp_peer(*FAR_FIRST[k]), me.t), device_id_type=MESH,
+                src_ref=ret_away.at[part, pl.ds(k * BLK, BLK), :], dst_ref=landing.at[mine_there, :],
+                send_sem=dp_send.at[row, k], recv_sem=dp_recv.at[row, k],
+                device_id=(me.dp_peer(*FAR_FIRST[k]), core), device_id_type=MESH,
             )
             copy.start()
-            back.append(copy)
+            copies.append(copy)
+        return copies
+
+    for part in range(2):
+        for batch in range(2):
+            block = jnp.dot(unpick, found[part][batch * BATCH : (batch + 1) * BATCH], preferred_element_type=F32)
+            ret_away[part, batch * 128 : (batch + 1) * 128, :] = block.astype(BF)
+        if part == 0:
+            back = give(0, 1, me.t, slots.at[0]) + give(0, 2, me.other, slots.at[1])
+        else:
+            back_tails = give(1, 4, me.t, tails)
 
     @pl.loop(0, ROWS // PBLK)
     def _(block):
@@ -433,31 +459,24 @@
         position = (iota((PBLK, SLOTS), 0) + base).astype(F32)
         written = jnp.where(position == end_row[0:1, :], 1.0, 0.0)
         hit = jnp.max(written, axis=1, keepdims=True) > 0.5
-        fresh = jnp.dot(written.astype(BF), compact[:, 128:384], preferred_element_type=F32)
+        fresh = jnp.dot(written.astype(BF), fresh_kv[...], preferred_element_type=F32)
         cache[0, span, :] = jnp.where(hit, fresh[:, 0:128], cache[0, span, :].astype(F32)).astype(BF)
         cache[1, span, :] = jnp.where(hit, fresh[:, 128:256], cache[1, span, :].astype(F32)).astype(BF)
 
     loads[9].wait()
     for copy in back:
         copy.wait_recv()
-    slots[HOME:, :] = landing[...]
-
-    def assemble(core):
-        rows = pl.ds(pl.multiple_of(core * 128, 128), 128)
-        return jnp.dot(scat[rows, :], slots[:, 0:128], preferred_element_type=F32).astype(BF)
-
-    attended[2] = assemble(1 - me.c)
-    swapped = to_core(attended.at[2], attended.at[1], 3)
-    attended[0] = assemble(me.c)
-    for half in range(2):
-        own[0, half] = jnp.dot(attended[0], wo[0, :, half * HALF : (half + 1) * HALF], preferred_element_type=F32)
+    swapped.wait_recv()
+    my_half = pl.ds(pl.multiple_of(me.c * 128, 128), 128)
+    for which in range(2):
+        attended[which] = jnp.dot(scat[my_half, :], slots[which], preferred_element_type=F32).astype(BF)
+    shared += [to_core(gu_hbm, gu.at[1], 1), to_core(wd_hbm, wd.at[1], 2)]
     shared[0].wait_recv()
-    swapped.wait_recv()
-    shared += [to_core(gu_hbm, gu.at[1], 1), to_core(wd_hbm, wd.at[1], 2)]
 
     def out_product(half):
         columns = pl.ds(half * HALF, HALF)
-        return own[0, half] + jnp.dot(attended[1], wo[1, :, columns], preferred_element_type=F32)
+        value = jnp.dot(attended[0], wo[0, :, columns], preferred_element_type=F32)
+        return value + jnp.dot(attended[1], wo[1, :, columns], preferred_element_type=F32)
 
     total, drain_first = reduce_z(
         me, out_product, own.at[0], ring_out.at[0], ring_in.at[0], rs_send.at[0], rs_recv.at[0]
@@ -473,12 +492,14 @@
     begin, finish_mlp, _, drain_mlp = gather_z(me, gathered_mlp, row_of_chip, ag_send.at[1], ag_recv.at[1])
     begin()
     spread_sel = sel[...].astype(F32)
-    tail = slots[:, 128:256].astype(F32)
+    for copy in back_tails:
+        copy.wait_recv()
+    tail = tails[...].astype(F32)
     for head in range(2):
         lse = tail[:, 2 * head : 2 * head + 1] + tail[:, 2 * head + 1 : 2 * head + 2]
         lse_out[head : head + 1, :] = jnp.sum(spread_sel * lse, axis=0, keepdims=True)
     drain_first()
-    for copy in sent + back:
+    for copy in sent[0] + sent[1] + back + back_tails:
         copy.wait_send()
     loads[11].wait()
     loads[12].wait()
@@ -511,7 +532,10 @@
 
 
 def store_kernel(hidden, lse, cache, hidden_out, lse_out, cache_out, sems):
-    pairs = [(cache.at[0], cache_out.at[0]), (cache.at[1], cache_out.at[1]), (hidden, hidden_out), (lse, lse_out)]
+    pairs = [(hidden, hidden_out), (lse, lse_out)]
+    for part in range(8):
+        at = (part // 4, pl.ds(part % 4 * (ROWS // 4), ROWS // 4))
+        pairs.append((cache.at[at], cache_out.at[at]))
     copies = [pltpu.make_async_copy(src, dst, sems.at[i]) for i, (src, dst) in enumerate(pairs)]
     for copy in copies:
         copy.start()
@@ -535,16 +559,16 @@
         scratch_shapes=[
             pltpu.VMEM((BLK, D), BF), pltpu.VMEM((16, 128), BF), pltpu.VMEM((16, 128), BF), pltpu.VMEM((3, 32, 128), I32),
             pltpu.VMEM((D, 384), BF), pltpu.VMEM((2, 128, D), BF), pltpu.VMEM((2, 2, D, FFL), BF), pltpu.VMEM((2, FFL, D), BF),
-            pltpu.VMEM((2, REQ, HALF), BF), pltpu.VMEM((2, 128, HALF), BF), pltpu.VMEM((REQ, 384), BF), pltpu.VMEM((SLOTS, 384), BF),
+            pltpu.VMEM((2, REQ, HALF), BF), pltpu.VMEM((2, 128, HALF), BF), pltpu.VMEM((REQ, 384), BF), pltpu.VMEM((SLOTS, 128), BF), pltpu.VMEM((SLOTS, 256), BF),
             pltpu.VMEM((NDP * BLK, 384), BF), pltpu.VMEM((SLOTS, REQ), BF), pltpu.VMEM((SLOTS, REQ), BF), pltpu.VMEM((REQ, SLOTS), BF),
             pltpu.VMEM((HOME, 128), F32), pltpu.VMEM((HOME, 128), F32), pltpu.VMEM((8, SLOTS), F32),
             pltpu.VMEM((2 * BATCH, NDP * BLK), BF), pltpu.VMEM((2 * BATCH, 128), F32), pltpu.VMEM((2 * BATCH, 128), F32),
-            pltpu.VMEM((2 * BATCH, 384), BF), pltpu.VMEM((REQ, 128), F32), pltpu.VMEM((REQ, 128), F32),
+            pltpu.VMEM((2 * BATCH, 128), BF), pltpu.VMEM((2 * BATCH, 256), BF), pltpu.VMEM((REQ, 128), F32), pltpu.VMEM((REQ, 128), F32),
             pltpu.VMEM((4 * BATCH, 128), BF), pltpu.VMEM((4 * BATCH, ROWS), F32),
-            pltpu.VMEM((2, 8 * BLK, 256), BF), pltpu.VMEM((NDP * BLK, 256), BF),
-            pltpu.VMEM((SLOTS, 256), BF), pltpu.VMEM((3, 128, 128), BF), pltpu.VMEM((2, 128, FFL), BF), pltpu.VMEM((BLK, D), BF),
+            pltpu.VMEM((2, NDP * BLK, 128), BF),
+            pltpu.VMEM((2, SLOTS, 128), BF), pltpu.VMEM((SLOTS, 128), BF), pltpu.VMEM((2, 128, 128), BF), pltpu.VMEM((2, 128, FFL), BF), pltpu.VMEM((BLK, D), BF),
             pltpu.VMEM((2, 2, 128, HALF), F32), pltpu.VMEM((2, 2, 7, BLK, HALF), BF), pltpu.VMEM((2, 2, 7, BLK, HALF), BF),
-            DMA((2, 15)), DMA((2, 15)), DMA((2, 2, 7)), DMA((2, 2, 7)), DMA((16,)), DMA((16,)),
+            DMA((5, 15)), DMA((5, 15)), DMA((2, 2, 7)), DMA((2, 2, 7)), DMA((16,)), DMA((16,)),
             DMA((2, 2, 7)), DMA((2, 2, 7)), DMA((4,)), DMA((4,)), DMA((13,)),
         ],
         compiler_params=pltpu.CompilerParams(collective_id=0, has_side_effects=True, vmem_limit_bytes=54 << 20),
@@ -558,7 +582,7 @@
         out_shape=results,
         in_specs=[VMEM_SPEC] * 3,
         out_specs=(ANY_SPEC,) * 3,
-        scratch_shapes=[DMA((4,))],
+        scratch_shapes=[DMA((10,))],
         name="store_results",
     )(*(pltpu.with_memory_space_constraint(value, pltpu.VMEM) for value in held))
     return hidden_states, lse.T, kv_updated

time: 69.4 us -> 69 us (level)
  no operation moved by 1% of the time
where the time goes in v6:
time: 69 us; the launch traced here: 68.9 us
  Pallas kernels  68.3 us (99%)
    pallas_call x1, Pallas kernels, on_device(): pl.pallas_call(layer_kernel, out_shape=(pltpu.VMEM((BLK, D), BF), pltpu.V...  66.9 us
    pallas_call x1, Pallas kernels, on_device(): pl.pallas_call(store_kernel, out_shape=results, in_specs=[VMEM_SPEC] * 3,...  1.42 us

profile of v6, /device:TPU:32, one launch (start us, length us, event | category | flops | bytes accessed | tf_op | source)
XLA Modules:
  0.0 68.9 jit_solution(13575944943698770190)
XLA Ops:
  0.6 66.9 %decode_layer.1 = (bf16[16,2048]{1,0:T(8,128)(2,1)S(1)}, f32[2,256]{1,0:T(2,128)S(1)}, bf16[2,4096,128]{2,1,0:T(8,128)(2,1)S(1)}) custom-call(bf16[16,2048]{1,0:T(8,128)(2,1)} %tokens_hbm.1, bf16[16,128]{1,0:T(8,128)(2,1)} %bitcast.9, bf16[16,128]{1,0:T(8,128)(2,1)} %bitcast.10, s32[32,128]{1,0:T(8,128)} %bitcast.6, s32[32,128]{1,0:T(8,128)} %bitcast.7, ...), custom_call_target="tpu_custom_call" | custom-call | tf_op jit(solution)/shard_map/decode_layer/pallas_call | solution.py:554
  67.5 1.4 %store_results.1 = (bf16[16,2048]{1,0:T(8,128)(2,1)}, f32[2,256]{1,0:T(2,128)}, bf16[2,4096,128]{2,1,0:T(8,128)(2,1)}) custom-call(bf16[16,2048]{1,0:T(8,128)(2,1)S(1)} %get-tuple-element.9.hidden, f32[2,256]{1,0:T(2,128)S(1)} %get-tuple-element.10.lse, bf16[2,4096,128]{2,1,0:T(8,128)(2,1)S(1)} %get-tuple-element.11.cache), custom_call_target="tpu_custom_call" | custom-call | tf_op jit(solution)/shard_map/store_results/pallas_call | solution.py:580

commit v7 on v6

--- a/solution.py
+++ b/solution.py
@@ -119,9 +119,9 @@
         message(way, index).wait_recv()
         distance, half, _ = kinds(way)[index]
         if distance == 2:
+            start(way, 4 + half)
             if half == way:
                 start(way, 6)
-            start(way, 4 + half)
         sibling((me.z + NZ - signs[way] * distance) % NZ, half)
 
     def finish():
@@ -168,7 +168,7 @@
     for half in range(2):
         own[half] = product(half)
         go(half, 2, mine(4 * signs[half], half))
-        for way in range(2):
+        for way in (1 - half, half):
             go(way, half, mine(3 * signs[way], half))
     for half in range(2):
         for way in range(2):
@@ -501,11 +501,11 @@
     drain_first()
     for copy in sent[0] + sent[1] + back + back_tails:
         copy.wait_send()
+    finish_mlp()
     loads[11].wait()
     loads[12].wait()
     shared[1].wait_recv()
     shared[2].wait_recv()
-    finish_mlp()
     for core in range(2):
         for tile in range(FFL // 256):
             columns = pl.ds(tile * 256, 256)

time: 69 us -> 69.1 us (level)
  no operation moved by 1% of the time
where the time goes in v7:
time: 69.1 us; the launch traced here: 68.5 us
  Pallas kernels  67.8 us (98%)
    pallas_call x1, Pallas kernels, on_device(): pl.pallas_call(layer_kernel, out_shape=(pltpu.VMEM((BLK, D), BF), pltpu.V...  66.4 us
    pallas_call x1, Pallas kernels, on_device(): pl.pallas_call(store_kernel, out_shape=results, in_specs=[VMEM_SPEC] * 3,...  1.42 us

profile of v7, /device:TPU:32, one launch (start us, length us, event | category | flops | bytes accessed | tf_op | source)
XLA Modules:
  0.0 68.5 jit_solution(2384125284428689519)
XLA Ops:
  0.6 66.4 %decode_layer.1 = (bf16[16,2048]{1,0:T(8,128)(2,1)S(1)}, f32[2,256]{1,0:T(2,128)S(1)}, bf16[2,4096,128]{2,1,0:T(8,128)(2,1)S(1)}) custom-call(bf16[16,2048]{1,0:T(8,128)(2,1)} %tokens_hbm.1, bf16[16,128]{1,0:T(8,128)(2,1)} %bitcast.9, bf16[16,128]{1,0:T(8,128)(2,1)} %bitcast.10, s32[32,128]{1,0:T(8,128)} %bitcast.6, s32[32,128]{1,0:T(8,128)} %bitcast.7, ...), custom_call_target="tpu_custom_call" | custom-call | tf_op jit(solution)/shard_map/decode_layer/pallas_call | solution.py:554
  67.1 1.4 %store_results.1 = (bf16[16,2048]{1,0:T(8,128)(2,1)}, f32[2,256]{1,0:T(2,128)}, bf16[2,4096,128]{2,1,0:T(8,128)(2,1)}) custom-call(bf16[16,2048]{1,0:T(8,128)(2,1)S(1)} %get-tuple-element.9.hidden, f32[2,256]{1,0:T(2,128)S(1)} %get-tuple-element.10.lse, bf16[2,4096,128]{2,1,0:T(8,128)(2,1)S(1)} %get-tuple-element.11.cache), custom_call_target="tpu_custom_call" | custom-call | tf_op jit(solution)/shard_map/store_results/pallas_call | solution.py:580
